TPU v7x, 32 devices: a whole 2x2x4 slice. The times are simulated.
32 devices in a mesh: seq: 4 (over z), fsdp: 8 (over y, x, core).
Axes of the slice: x: 2, y: 2, z: 4, core: 2. Of those that a mesh axis runs over, the one named last changes fastest.
Arguments:
- tokens: bfloat16 [8, 512, 768], P('fsdp', 'seq'), may hold values from -6 to 6
- positions: int32 [8, 512], P('fsdp', 'seq'), may hold values from 0 to 5117, as said below
- norm1_gain: bfloat16 [768], P('fsdp'), may hold values from 0.5 to 1.5
- qkv_weight: bfloat16 [768, 2304], P('fsdp'), may hold values from -0.57735027 to 0.57735027, as said below
- out_weight: bfloat16 [768, 768], P('fsdp'), may hold values from -6 to 6
- norm2_gain: bfloat16 [768], P('fsdp'), may hold values from 0.5 to 1.5
- in_weight: bfloat16 [768, 2304], P('fsdp'), may hold values from -0.21875 to 0.21875
- down_weight: bfloat16 [1152, 768], P(None, 'fsdp'), may hold values from -0.1875 to 0.1875
- cotangent: bfloat16 [8, 512, 768], P('fsdp', 'seq'), may hold values from -6 to 6
Outputs:
- block_out: bfloat16 [8, 512, 768], P('fsdp', 'seq')
- input_grad: bfloat16 [8, 512, 768], P('fsdp', 'seq')
- qkv_weight_grad: float32 [768, 2304], P('fsdp')
- out_weight_grad: float32 [768, 768], P('fsdp')
- in_weight_grad: float32 [768, 2304], P('fsdp')
- down_weight_grad: float32 [1152, 768], P(None, 'fsdp')
- norm1_gain_grad: float32 [768], P('fsdp')
- norm2_gain_grad: float32 [768], P('fsdp')
Inputs may be any that keep to these rules, and one draw needn't show every extreme that they name: Along each sequence the positions rise by 1 or 2 from one token to the next. `qkv_weight`: A projection matrix; every entry lies within 16 / sqrt(768) of zero.
All inputs are finite; a program needn't handle non-finite values.
Results may differ from a plain program's by a relative error of at most 0.019.
Values may be sent and summed in bfloat16 or wider, within the bound.
A program may use at most 128 MiB of HBM per device.

v0:
```python
import jax
import jax.numpy as jnp
from jax import lax
from jax.sharding import PartitionSpec as P

HEADS = 12
HEAD_DIM = 64


eps = 1e-05
theta = 160000.0


def layer_norm(values, gain_vec):
    middle = jnp.mean(values, axis=-1, keepdims=True)
    centred = values - middle
    inverse = lax.rsqrt(jnp.mean(centred * centred, axis=-1, keepdims=True) + eps)
    scaled = centred * inverse
    return (scaled * gain_vec, scaled, inverse)


def norm_back(upstream, scaled, inverse, gain_vec):
    gain_grad = jnp.sum(upstream * scaled, axis=0)
    weighted = upstream * gain_vec
    result = inverse * (
        weighted
        - jnp.mean(weighted, axis=-1, keepdims=True)
        - scaled * jnp.mean(weighted * scaled, axis=-1, keepdims=True)
    )
    return (result, gain_grad)


def rotary_tables(positions, head_size):
    half_dim = head_size // 2
    frequency = theta ** (-jnp.arange(half_dim, dtype=jnp.float32) / half_dim)
    angles = positions.astype(jnp.float32)[..., None] * frequency
    return (jnp.cos(angles)[..., None, :], jnp.sin(angles)[..., None, :])


def rotate(values, cosine_table, sine_table):
    half_dim = values.shape[-1] // 2
    first_half = values[..., :half_dim]
    second_half = values[..., half_dim:]
    return jnp.concatenate(
        [
            first_half * cosine_table - second_half * sine_table,
            second_half * cosine_table + first_half * sine_table,
        ],
        axis=-1,
    )


def rotate_back(values, cosine_table, sine_table):
    half_dim = values.shape[-1] // 2
    first_half = values[..., :half_dim]
    second_half = values[..., half_dim:]
    return jnp.concatenate(
        [
            first_half * cosine_table + second_half * sine_table,
            second_half * cosine_table - first_half * sine_table,
        ],
        axis=-1,
    )


def gelu_slope(values):
    return (
        0.5 * (1.0 + lax.erf(values * 0.7071067811865476))
        + values * jnp.exp(-0.5 * values * values) * 0.3989422804014327
    )


def local(
    tokens,
    positions,
    norm1_gain,
    qkv_weight,
    out_weight,
    norm2_gain,
    in_weight,
    down_weight,
    cotangent,
):
    f32 = jnp.float32
    low = jnp.bfloat16
    groups = lax.axis_size("seq")
    seq_dev, span_len, model_width = tokens.shape
    row_count = seq_dev * span_len
    local_heads = HEADS // groups
    group_width = local_heads * HEAD_DIM
    length = span_len * groups
    block_rows = min(512, length)
    block_count = length // block_rows
    score_scale = HEAD_DIM ** (-0.5)
    gathered = (
        lax.all_gather(qkv_weight, "fsdp", axis=0, tiled=True),
        lax.all_gather(out_weight, "fsdp", axis=0, tiled=True),
        lax.all_gather(in_weight, "fsdp", axis=0, tiled=True),
        lax.all_gather(down_weight, "fsdp", axis=1, tiled=True),
        lax.all_gather(norm1_gain, "fsdp", axis=0, tiled=True),
        lax.all_gather(norm2_gain, "fsdp", axis=0, tiled=True),
    )
    w_qkv, w_out, w_in, w_down, gain_one, gain_two = gathered
    gain_one = gain_one.astype(f32)
    gain_two = gain_two.astype(f32)
    inputs = tokens.reshape(row_count, model_width).astype(f32)
    normed_one, scaled_one, inverse_one = layer_norm(inputs, gain_one)
    normed_one = normed_one.astype(low)
    projected = jnp.dot(normed_one, w_qkv, preferred_element_type=f32).reshape(
        seq_dev, span_len, 3, HEADS, HEAD_DIM
    )
    cosine_table, sine_table = rotary_tables(positions, HEAD_DIM)
    queries = rotate(projected[:, :, 0], cosine_table, sine_table)
    key_part = rotate(projected[:, :, 1], cosine_table, sine_table)
    packed = jnp.stack([queries, key_part, projected[:, :, 2]], axis=2).astype(low)
    packed = packed.reshape(seq_dev, span_len, 3, groups, group_width)
    heads = lax.all_to_all(packed, "seq", split_axis=3, concat_axis=1, tiled=True)
    heads = heads.reshape(seq_dev, length, 3, local_heads, HEAD_DIM)
    query_rows = heads[:, :, 0]
    key_rows = heads[:, :, 1]
    value_rows = heads[:, :, 2]
    query_blocks = jnp.swapaxes(
        query_rows.reshape(seq_dev, block_count, block_rows, local_heads, HEAD_DIM), 0, 1
    )

    def attend(query_block):
        scores = (
            jnp.einsum("bqhd,bkhd->bhqk", query_block, key_rows, preferred_element_type=f32)
            * score_scale
        )
        totals = jax.nn.logsumexp(scores, axis=-1)
        probs_low = jnp.exp(scores - totals[..., None]).astype(low)
        result = jnp.einsum("bhqk,bkhd->bqhd", probs_low, value_rows, preferred_element_type=f32)
        return (result.astype(low), totals)

    attended, totals = lax.map(attend, query_blocks)
    attended = jnp.swapaxes(attended, 0, 1).reshape(seq_dev, length, local_heads, HEAD_DIM)
    outgoing = attended.reshape(seq_dev, length, 1, group_width)
    returned = lax.all_to_all(outgoing, "seq", split_axis=1, concat_axis=2, tiled=True)
    mixed_heads = returned.reshape(row_count, model_width)
    residual = inputs + jnp.dot(mixed_heads, w_out, preferred_element_type=f32)
    normed_two, scaled_two, inverse_two = layer_norm(residual, gain_two)
    normed_two = normed_two.astype(low)
    lifted = jnp.dot(normed_two, w_in, preferred_element_type=f32)
    ff_size = lifted.shape[1] // 2
    act_input = lifted[:, :ff_size]
    gate_part = lifted[:, ff_size:]
    activated = jax.nn.gelu(act_input, approximate=False)
    gated = (activated * gate_part).astype(low)
    block_out = (residual + jnp.dot(gated, w_down, preferred_element_type=f32)).astype(low)
    regathered = (
        lax.all_gather(qkv_weight, "fsdp", axis=0, tiled=True),
        lax.all_gather(out_weight, "fsdp", axis=0, tiled=True),
        lax.all_gather(in_weight, "fsdp", axis=0, tiled=True),
        lax.all_gather(down_weight, "fsdp", axis=1, tiled=True),
        lax.all_gather(norm1_gain, "fsdp", axis=0, tiled=True),
        lax.all_gather(norm2_gain, "fsdp", axis=0, tiled=True),
    )
    w_qkv, w_out, w_in, w_down, gain_low_one, gain_low_two = regathered
    gain_one = gain_low_one.astype(f32)
    gain_two = gain_low_two.astype(f32)
    upstream = cotangent.reshape(row_count, model_width)
    gated_grad = jnp.dot(upstream, w_down.T, preferred_element_type=f32)
    lifted_grad = jnp.concatenate(
        [gated_grad * gate_part * gelu_slope(act_input), gated_grad * activated], axis=1
    ).astype(low)
    normed_two_grad = jnp.dot(lifted_grad, w_in.T, preferred_element_type=f32)
    residual_part, gain_two_grad = norm_back(normed_two_grad, scaled_two, inverse_two, gain_two)
    residual_grad = upstream.astype(f32) + residual_part
    residual_low = residual_grad.astype(low)
    mixed_grad = jnp.dot(residual_low, w_out.T, preferred_element_type=f32).astype(low)
    grad_outgoing = mixed_grad.reshape(seq_dev, span_len, groups, group_width)
    grad_heads = lax.all_to_all(grad_outgoing, "seq", split_axis=2, concat_axis=1, tiled=True)
    grad_heads = grad_heads.reshape(seq_dev, length, local_heads, HEAD_DIM)
    delta_rows = jnp.sum(grad_heads.astype(f32) * attended.astype(f32), axis=-1)
    grad_blocks = jnp.swapaxes(
        grad_heads.reshape(seq_dev, block_count, block_rows, local_heads, HEAD_DIM), 0, 1
    )
    delta_blocks = jnp.swapaxes(
        jnp.swapaxes(delta_rows.reshape(seq_dev, block_count, block_rows, local_heads), 0, 1), 2, 3
    )

    def attend_back(carry, block_inputs):
        key_total, value_total = carry
        query_block, grad_block, delta_block, total_block = block_inputs
        scores = (
            jnp.einsum("bqhd,bkhd->bhqk", query_block, key_rows, preferred_element_type=f32)
            * score_scale
        )
        probs = jnp.exp(scores - total_block[..., None])
        probs_low = probs.astype(low)
        value_total = value_total + jnp.einsum(
            "bhqk,bqhd->bkhd", probs_low, grad_block, preferred_element_type=f32
        )
        prob_grad = jnp.einsum(
            "bqhd,bkhd->bhqk", grad_block, value_rows, preferred_element_type=f32
        )
        score_grad = (probs * (prob_grad - delta_block[..., None])).astype(low)
        query_grad = (
            jnp.einsum("bhqk,bkhd->bqhd", score_grad, key_rows, preferred_element_type=f32)
            * score_scale
        ).astype(low)
        key_total = key_total + jnp.einsum(
            "bhqk,bqhd->bkhd", score_grad, query_block, preferred_element_type=f32
        )
        return ((key_total, value_total), query_grad)

    zeros_state = jnp.zeros((seq_dev, length, local_heads, HEAD_DIM), f32)
    (key_total, value_total), query_grads = lax.scan(
        attend_back, (zeros_state, zeros_state), (query_blocks, grad_blocks, delta_blocks, totals)
    )
    query_grad = jnp.swapaxes(query_grads, 0, 1).reshape(seq_dev, length, group_width)
    key_grad = (key_total * score_scale).astype(low).reshape(seq_dev, length, group_width)
    value_grad = value_total.astype(low).reshape(seq_dev, length, group_width)
    grads_outgoing = jnp.stack([query_grad, key_grad, value_grad], axis=2)[:, :, :, None, :]
    grads_returned = lax.all_to_all(grads_outgoing, "seq", split_axis=1, concat_axis=3, tiled=True)
    grads_returned = grads_returned.reshape(seq_dev, span_len, 3, HEADS, HEAD_DIM).astype(f32)
    qkv_grad = jnp.stack(
        [
            rotate_back(grads_returned[:, :, 0], cosine_table, sine_table),
            rotate_back(grads_returned[:, :, 1], cosine_table, sine_table),
            grads_returned[:, :, 2],
        ],
        axis=2,
    )
    qkv_grad = qkv_grad.reshape(row_count, 3 * model_width).astype(low)
    normed_one_grad = jnp.dot(qkv_grad, w_qkv.T, preferred_element_type=f32)
    input_part, gain_one_grad = norm_back(normed_one_grad, scaled_one, inverse_one, gain_one)
    input_grad = (residual_grad + input_part).astype(low).reshape(seq_dev, span_len, model_width)
    gain_terms = (gain_one_grad, gain_two_grad)
    terms = (
        jnp.dot(normed_one.T, qkv_grad, preferred_element_type=f32),
        jnp.dot(mixed_heads.T, residual_low, preferred_element_type=f32),
        jnp.dot(normed_two.T, lifted_grad, preferred_element_type=f32),
        jnp.dot(gated.T, upstream, preferred_element_type=f32),
        gain_terms[0],
        gain_terms[1],
    )
    pieces = (
        lax.psum_scatter(terms[0], "fsdp", scatter_dimension=0, tiled=True),
        lax.psum_scatter(terms[1], "fsdp", scatter_dimension=0, tiled=True),
        lax.psum_scatter(terms[2], "fsdp", scatter_dimension=0, tiled=True),
        lax.psum_scatter(terms[3], "fsdp", scatter_dimension=1, tiled=True),
        lax.psum_scatter(terms[4], "fsdp", scatter_dimension=0, tiled=True),
        lax.psum_scatter(terms[5], "fsdp", scatter_dimension=0, tiled=True),
    )
    parts = (
        lax.psum_scatter(
            pieces[0].astype(jnp.bfloat16), "seq", scatter_dimension=0, tiled=True
        ).astype(jnp.float32),
        lax.psum_scatter(
            pieces[1].astype(jnp.bfloat16), "seq", scatter_dimension=0, tiled=True
        ).astype(jnp.float32),
        lax.psum_scatter(
            pieces[2].astype(jnp.bfloat16), "seq", scatter_dimension=0, tiled=True
        ).astype(jnp.float32),
        lax.psum_scatter(
            pieces[3].astype(jnp.bfloat16), "seq", scatter_dimension=1, tiled=True
        ).astype(jnp.float32),
        lax.psum_scatter(
            pieces[4].astype(jnp.bfloat16), "seq", scatter_dimension=0, tiled=True
        ).astype(jnp.float32),
        lax.psum_scatter(
            pieces[5].astype(jnp.bfloat16), "seq", scatter_dimension=0, tiled=True
        ).astype(jnp.float32),
    )
    summed = (
        lax.all_gather(parts[0].astype(jnp.bfloat16), "seq", axis=0, tiled=True).astype(
            jnp.float32
        ),
        lax.all_gather(parts[1].astype(jnp.bfloat16), "seq", axis=0, tiled=True).astype(
            jnp.float32
        ),
        lax.all_gather(parts[2].astype(jnp.bfloat16), "seq", axis=0, tiled=True).astype(
            jnp.float32
        ),
        lax.all_gather(parts[3].astype(jnp.bfloat16), "seq", axis=1, tiled=True).astype(
            jnp.float32
        ),
        lax.all_gather(parts[4].astype(jnp.bfloat16), "seq", axis=0, tiled=True).astype(
            jnp.float32
        ),
        lax.all_gather(parts[5].astype(jnp.bfloat16), "seq", axis=0, tiled=True).astype(
            jnp.float32
        ),
    )
    return (
        block_out.reshape(seq_dev, span_len, model_width),
        input_grad,
        summed[0],
        summed[1],
        summed[2],
        summed[3],
        summed[4],
        summed[5],
    )


def solution(mesh):
    in_specs = (
        P("fsdp", "seq", None),
        P("fsdp", "seq"),
        P("fsdp"),
        P("fsdp", None),
        P("fsdp", None),
        P("fsdp"),
        P("fsdp", None),
        P(None, "fsdp"),
        P("fsdp", "seq", None),
    )
    out_specs = (
        P("fsdp", "seq", None),
        P("fsdp", "seq", None),
        P("fsdp", None),
        P("fsdp", None),
        P("fsdp", None),
        P(None, "fsdp"),
        P("fsdp"),
        P("fsdp"),
    )
    return jax.shard_map(local, mesh=mesh, in_specs=in_specs, out_specs=out_specs, check_vma=False)
```

profile of v0, /device:TPU:0, one launch (start us, length us, event | category | flops | bytes accessed | tf_op | source)
XLA Modules:
  0.0 489.6 jit_solution(12036840399194156989)
XLA Ops:
  9.4 1.3 fusion.60
  11.4 0.8 dynamic-update-slice
  12.2 0.8 dynamic-update-slice.1
  13.1 16.1 %all-reduce.10 = (bf16[768]{0:T(1024)(128)(2,1)S(1)}, bf16[768]{0:T(1024)(128)(2,1)}) all-reduce(bf16[768]{0:T(1024)(128)(2,1)S(1)} %dynamic-update-slice, bf16[768]{0:T(1024)(128)(2,1)S(1)} %dynamic-update-slice.1), channel_id=1, replica_groups=mesh['seq'=4,'fsdp'=8] {'fsdp'}, use_global_device_ids=true, to_apply=%add | all-reduce | flops 1536 | bytes 6144
  29.2 1.0 convert_reduce_fusion
  30.3 1.1 fusion.32
  32.8 13.7 %all-gather.5.cloned.1.call-done = bf16[768,2304]{1,0:T(8,128)(2,1)} async-done(((bf16[96,2304]{1,0:T(8,128)(2,1)}), bf16[768,2304]{1,0:T(8,128)(2,1)}) %all-gather.5.cloned.1.call-update) | async-done | bytes 3538960 | tf_op jit(solution)/shard_map/all_gather | solution.py:96
  46.6 4.5 copy.88
  51.1 2.1 convolution_bitcast_fusion
  53.5 0.9 pad_maximum_fusion
  54.4 4.6 all-to-all-start
  59.6 15.7 %all-to-all-done = bf16[1,128,3,4,192]{1,4,2,0,3:T(8,128)(2,1)S(1)} async-done(((bf16[1,128,3,4,192]{1,4,2,0,3:T(8,128)(2,1)}), bf16[1,128,3,4,192]{1,4,2,0,3:T(8,128)(2,1)S(1)}, u32[]{:S(2)}, u32[]{:S(2)}) %all-to-all-start) | async-done | bytes 589856 | tf_op jit(solution)/shard_map/all_to_all | solution.py:117
  75.8 1.0 reshape.462
  76.8 1.7 multiply_reduce_fusion
  79.0 1.6 convolution_convert_fusion.2
  80.7 1.1 copy.94
  82.2 3.9 reduce.6
  86.1 2.0 reshape.502
  88.1 3.4 all-to-all-start.1
  92.4 6.4 %all-to-all-done.1 = bf16[4,2,12288]{2,1,0:T(2,128)(2,1)S(1)} async-done(((bf16[4,2,12288]{2,1,0:T(2,128)(2,1)}), bf16[4,2,12288]{2,1,0:T(2,128)(2,1)S(1)}, u32[]{:S(2)}, u32[]{:S(2)}) %all-to-all-start.1) | async-done | bytes 196640 | tf_op jit(solution)/shard_map/all_to_all | solution.py:139
  98.7 1.1 reshape.503
  99.8 1.9 copy.95
  101.7 1.0 all_to_all.44
  103.3 1.8 fusion.62
  106.5 1.7 all-gather.9.cloned.1.call-done
  108.1 3.7 fusion.58
  111.9 24.5 %all-gather.11.cloned.1.call-done = bf16[1152,768]{0,1:T(8,128)(2,1)} async-done(((bf16[1152,96]{0,1:T(8,128)(2,1)}), bf16[1152,768]{0,1:T(8,128)(2,1)}) %all-gather.11.cloned.1.call-update) | async-done | bytes 1769488 | tf_op jit(solution)/shard_map/all_gather | solution.py:99
  136.3 4.6 multiply_convert_fusion.1
  141.0 1.9 multiply_reduce_fusion.1
  143.9 1.9 fusion.49
  145.9 1.3 multiply_convert_fusion.2
  147.9 3.3 fusion.42
  151.3 5.2 %fusion.36 = f32[768,2304]{1,0:T(8,128)} fusion(bf16[128,1152]{1,0:T(8,128)(2,1)} %copy-done.13, bf16[128,1152]{1,0:T(8,128)(2,1)} %copy-done.14, f32[128,768]{1,0:T(8,128)S(1)} %get-tuple-element.98, f32[768]{0:T(1024)S(1)} %convert_element_type.222, f32[128]{0:T(128)} %add_rsqrt_fusion, f32[128]{0:T(128)} %copy-done.21), kind=kOutput, calls=%fused_computation.80 | convolution fusion | flops 454557696 | bytes 8065024 | tf_op jit(solution)/shard_map/dot_general | solution.py:234
  156.5 2.7 convolution_convert_fusion.1
  159.2 1.7 copy.97
  161.0 12.5 %all_to_all.54 = bf16[1,128,4,192]{1,3,0,2:T(8,128)(2,1)S(1)} all-to-all(bf16[1,128,4,192]{1,3,0,2:T(8,128)(2,1)} %bitcast.196), channel_id=1, replica_groups=mesh['seq'=4,'fsdp'=8] {'seq'}, dimensions={2} | all-to-all | bytes 393216 | tf_op jit(solution)/shard_map/all_to_all | solution.py:173
  175.0 1.7 reshape.470
  176.7 1.0 bitcast_convert_fusion
  177.6 1.0 copy.100
  178.6 1.9 reshape.473
  180.5 1.2 multiply_reduce_fusion.2
  181.7 1.9 multiply_convert_fusion
  186.1 28.2 %all_to_all.55 = bf16[1,512,3,1,192]{4,2,3,0,1:T(4,128)(2,1)S(1)} all-to-all(bf16[1,512,3,1,192]{4,2,3,0,1:T(4,128)(2,1)S(1)} %copy.105), channel_id=1, replica_groups=mesh['seq'=4,'fsdp'=8] {'seq'}, dimensions={1} | all-to-all | bytes 1179648 | tf_op jit(solution)/shard_map/all_to_all | solution.py:216
  216.3 4.2 fusion.46
  220.6 1.8 convert_element_type.251
  222.5 17.1 %reduce-scatter.23.cloned.1.call-done = f32[1152,96]{0,1:T(8,128)} async-done(((f32[1152,768]{0,1:T(8,128)}), f32[1152,96]{0,1:T(8,128)}) %reduce-scatter.23.cloned.1.call-update) | async-done | bytes 442384 | tf_op jit(solution)/shard_map/reduce_scatter | solution.py:243
  239.6 1.7 convert_element_type.255
  241.4 67.3 %reduce-scatter.19.cloned.1.call-done = f32[96,2304]{1,0:T(8,128)} async-done(((f32[768,2304]{1,0:T(8,128)}), f32[96,2304]{1,0:T(8,128)}) %reduce-scatter.19.cloned.1.call-update) | async-done | bytes 884752 | tf_op jit(solution)/shard_map/reduce_scatter | solution.py:242
  308.7 2.0 convert_element_type.253
  312.6 1.3 fusion.4
  313.9 3.4 fusion.31
  317.4 60.3 %reduce-scatter.11.cloned.1.call-done = f32[96,2304]{1,0:T(8,128)} async-done(((f32[768,2304]{1,0:T(8,128)}), f32[96,2304]{1,0:T(8,128)}) %reduce-scatter.11.cloned.1.call-update) | async-done | bytes 884752 | tf_op jit(solution)/shard_map/reduce_scatter | solution.py:240
  377.7 2.0 convert_element_type.249
  379.7 12.8 %all-reduce.9 = (bf16[768]{0:T(1024)(128)(2,1)S(1)}, bf16[768]{0:T(1024)(128)(2,1)S(1)}) all-reduce(f32[768]{0:T(1024)S(1)} %get-tuple-element.48, f32[768]{0:T(1024)S(1)} %copy-done.26), channel_id=10, replica_groups=mesh['seq'=4,'fsdp'=8] {'fsdp'}, use_global_device_ids=true, to_apply=%region_20.21.clone | all-reduce | flops 1536 | bytes 9216
  392.6 11.7 %all-reduce.12 = (bf16[96]{0:T(256)(128)(2,1)S(1)}, bf16[96]{0:T(256)(128)(2,1)S(1)}) all-reduce(bf16[96]{0:T(256)(128)(2,1)S(1)} %dynamic-slice.19, bf16[96]{0:T(256)(128)(2,1)S(1)} %dynamic-slice.18), channel_id=11, replica_groups=mesh['seq'=4,'fsdp'=8] {'seq'}, use_global_device_ids=true, to_apply=%region_21.22.clone | all-reduce | flops 192 | bytes 768
  404.9 8.3 %all-reduce.11 = (bf16[96]{0:T(256)(128)(2,1)S(1)}, bf16[96]{0:T(256)(128)(2,1)S(1)}) all-reduce(bf16[96]{0:T(256)(128)(2,1)S(1)} %dynamic-update-slice.2, bf16[96]{0:T(256)(128)(2,1)S(1)} %dynamic-update-slice.3), channel_id=1, replica_groups=mesh['seq'=4,'fsdp'=8] {'seq'}, use_global_device_ids=true, to_apply=%add.2 | all-reduce | flops 192 | bytes 768
  414.2 0.9 fusion.40
  415.1 13.9 %all_gather.49 = bf16[96,768]{1,0:T(8,128)(2,1)S(1)} all-gather(bf16[24,768]{1,0:T(8,128)(2,1)} %reduce-scatter.17.cloned.1.call-done), channel_id=1, replica_groups=mesh['seq'=4,'fsdp'=8] {'seq'}, dimensions={0}, use_global_device_ids=true | all-gather | bytes 184320 | tf_op jit(solution)/shard_map/all_gather | solution.py:271
  429.7 14.9 %all_gather.51 = bf16[1152,96]{0,1:T(8,128)(2,1)S(1)} all-gather(bf16[1152,24]{0,1:T(8,128)(2,1)} %reduce-scatter.25.cloned.1.call-done), channel_id=1, replica_groups=mesh['seq'=4,'fsdp'=8] {'seq'}, dimensions={1}, use_global_device_ids=true | all-gather | bytes 276480 | tf_op jit(solution)/shard_map/all_gather | solution.py:277
  445.4 17.3 %all_gather.50 = bf16[96,2304]{1,0:T(8,128)(2,1)S(1)} all-gather(bf16[24,2304]{1,0:T(8,128)(2,1)} %reduce-scatter.21.cloned.1.call-done), channel_id=1, replica_groups=mesh['seq'=4,'fsdp'=8] {'seq'}, dimensions={0}, use_global_device_ids=true | all-gather | bytes 552960 | tf_op jit(solution)/shard_map/all_gather | solution.py:274
  462.8 1.0 convert_element_type.254
  463.7 2.5 reduce-scatter.13.cloned.1.call-done
  466.2 15.6 %all_gather.48 = bf16[96,2304]{1,0:T(8,128)(2,1)S(1)} all-gather(bf16[24,2304]{1,0:T(8,128)(2,1)} %reduce-scatter.13.cloned.1.call-done), channel_id=1, replica_groups=mesh['seq'=4,'fsdp'=8] {'seq'}, dimensions={0}, use_global_device_ids=true | all-gather | bytes 552960 | tf_op jit(solution)/shard_map/all_gather | solution.py:268
  481.8 1.0 convert_element_type.250
  (138 shorter events, 20.1 us)
Async XLA Ops:
  7.2 39.4 %all-gather.5.cloned.1.call-start = ((), (), s32[]{:S(2)}) async-start(), calls=%async_computation.12 | async-start | bytes 3981312 | tf_op jit(solution)/shard_map/all_gather | solution.py:96
  7.9 95.4 %all-gather.7.cloned.1.call-start = ((), (), s32[]{:S(2)}) async-start(), calls=%async_computation.13 | async-start | bytes 1327104 | tf_op jit(solution)/shard_map/all_gather | solution.py:97
  8.6 99.5 %all-gather.9.cloned.1.call-start = ((), (), s32[]{:S(2)}) async-start(), calls=%async_computation.14 | async-start | bytes 3981312 | tf_op jit(solution)/shard_map/all_gather | solution.py:98
  30.2 20.8 %copy-start.19 = (f32[128]{0:T(128)}, f32[128]{0:T(128)S(1)}, u32[]{:S(2)}) copy-start(f32[128]{0:T(128)S(1)} %broadcast_multiply_fusion.5) | copy-start | bytes 1540
  31.4 19.7 %copy-start.23 = (f32[128]{0:T(128)}, f32[128]{0:T(128)S(1)}, u32[]{:S(2)}) copy-start(f32[128]{0:T(128)S(1)} %add_rsqrt_fusion.1) | copy-start | bytes 1540
  51.1 2.3 copy-start.15
  51.1 2.3 copy-start.17
  54.4 20.9 %all-to-all-start = ((bf16[1,128,3,4,192]{1,4,2,0,3:T(8,128)(2,1)}), bf16[1,128,3,4,192]{1,4,2,0,3:T(8,128)(2,1)S(1)}, u32[]{:S(2)}, u32[]{:S(2)}) async-start(bf16[1,128,3,4,192]{1,4,2,0,3:T(8,128)(2,1)} %pad_maximum_fusion), calls=%async_computation | async-start | bytes 1179648 | tf_op jit(solution)/shard_map/all_to_all | solution.py:117
  59.0 77.3 %all-gather.11.cloned.1.call-start = ((), (), s32[]{:S(2)}) async-start(), calls=%async_computation.15 | async-start | bytes 1990656 | tf_op jit(solution)/shard_map/all_gather | solution.py:99
  80.6 22.7 %copy-start.9 = (bf16[3,64,512]{2,1,0:T(8,128)(2,1)}, bf16[3,64,512]{2,1,0:T(8,128)(2,1)S(1)}, u32[]{:S(2)}) copy-start(bf16[3,64,512]{2,1,0:T(8,128)(2,1)S(1)} %convolution_convert_fusion.2) | copy-start | bytes 589828
  88.1 10.6 %all-to-all-start.1 = ((bf16[4,2,12288]{2,1,0:T(2,128)(2,1)}), bf16[4,2,12288]{2,1,0:T(2,128)(2,1)S(1)}, u32[]{:S(2)}, u32[]{:S(2)}) async-start(bf16[4,2,12288]{2,1,0:T(2,128)(2,1)} %reshape.502), calls=%async_computation.1 | async-start | bytes 393216 | tf_op jit(solution)/shard_map/all_to_all | solution.py:139
  91.5 129.1 %reduce-scatter.15.cloned.1.call-start = ((), (), s32[]{:S(2)}) async-start(), calls=%async_computation.18 | async-start | bytes 2654208 | tf_op jit(solution)/shard_map/reduce_scatter | solution.py:241
  105.2 0.6 copy-start.21
  136.3 4.6 copy-start.4
  136.3 4.6 copy-start.22
  136.3 4.6 copy-start.25
  140.9 2.2 copy-start.13
  140.9 2.2 copy-start.14
  140.9 2.0 copy-start.12
  141.0 2.9 copy-start.8
  143.1 0.7 copy-start.1
  145.8 93.8 %reduce-scatter.23.cloned.1.call-start = ((), (), s32[]{:S(2)}) async-start(), calls=%async_computation.22 | async-start | bytes 3981312 | tf_op jit(solution)/shard_map/reduce_scatter | solution.py:243
  147.2 0.7 copy-start.5
  151.2 157.4 %reduce-scatter.19.cloned.1.call-start = ((), (), s32[]{:S(2)}) async-start(), calls=%async_computation.20 | async-start | bytes 7962624 | tf_op jit(solution)/shard_map/reduce_scatter | solution.py:242
  156.5 221.2 %reduce-scatter.11.cloned.1.call-start = ((), (), s32[]{:S(2)}) async-start(), calls=%async_computation.16 | async-start | bytes 7962624 | tf_op jit(solution)/shard_map/reduce_scatter | solution.py:240
  173.5 0.7 copy-start.10
  180.5 3.1 copy-start.3
  183.7 1.0 copy-start.7
  215.2 0.7 copy-start.16
  215.3 0.7 copy-start.18
  215.4 0.9 copy-start
  215.4 0.9 copy-start.20
  215.4 0.9 copy-start.24
  220.5 92.1 %copy-start.6 = (bf16[128,1152]{1,0:T(8,128)(2,1)S(1)}, bf16[128,1152]{1,0:T(8,128)(2,1)}, u32[]{:S(2)}) copy-start(bf16[128,1152]{1,0:T(8,128)(2,1)} %copy-done.5) | copy-start | bytes 884740
  220.5 92.1 %copy-start.11 = (bf16[1152,768]{0,1:T(8,128)(2,1)S(1)}, bf16[1152,768]{0,1:T(8,128)(2,1)}, u32[]{:S(2)}) copy-start(bf16[1152,768]{0,1:T(8,128)(2,1)} %all-gather.11.cloned.1.call-done) | copy-start | bytes 5308420
  220.5 194.6 %reduce-scatter.17.cloned.1.call-start = ((), (), s32[]{:S(2)}) async-start(), calls=%async_computation.19 | async-start | bytes 184320 | tf_op jit(solution)/shard_map/reduce_scatter | solution.py:251
  222.4 207.3 %reduce-scatter.25.cloned.1.call-start = ((), (), s32[]{:S(2)}) async-start(), calls=%async_computation.23 | async-start | bytes 276480
  241.3 204.1 %reduce-scatter.21.cloned.1.call-start = ((), (), s32[]{:S(2)}) async-start(), calls=%async_computation.21 | async-start | bytes 552960 | tf_op jit(solution)/shard_map/reduce_scatter | solution.py:254
  310.7 155.6 %reduce-scatter.13.cloned.1.call-start = ((), (), s32[]{:S(2)}) async-start(), calls=%async_computation.17 | async-start | bytes 552960 | tf_op jit(solution)/shard_map/reduce_scatter | solution.py:248
  313.9 65.8 %copy-start.26 = (f32[768]{0:T(1024)S(1)}, f32[768]{0:T(1024)}, u32[]{:S(2)}) copy-start(f32[768]{0:T(1024)} %get-tuple-element.46) | copy-start | bytes 9220
  313.9 100.3 %copy-start.2 = (f32[128,768]{1,0:T(8,128)S(1)}, f32[128,768]{1,0:T(8,128)}, u32[]{:S(2)}) copy-start(f32[128,768]{1,0:T(8,128)} %copy-done.1) | copy-start | bytes 1179652
Sparse Core Ops, SparseCore 0:
  9.9 36.6 all-gather.4
  48.4 23.9 all-gather.6
  74.3 33.8 all-gather.8
  109.9 26.3 all-gather.10
  145.9 42.3 reduce-scatter.14
  191.6 47.9 reduce-scatter.22
  243.1 65.4 reduce-scatter.18
  312.2 65.4 reduce-scatter.10
  379.9 19.4 reduce-scatter.16
  401.6 17.8 reduce-scatter.24
  422.4 21.0 reduce-scatter.20
  446.2 19.9 reduce-scatter.12
where the time goes:
time: 491 us; the launch traced here: 490 us
  waiting for transfers between devices  212 us (43%)
  blocking collectives  151 us (31%)
  matrix products  43 us (9%)
  local copies, waits for them, and re-layouts  30.4 us (6%)
  other arithmetic  27.2 us (6%)
  between operations  17.3 us (4%)
  starting transfers between devices  8.59 us (2%)
    reduce_scatter x1, waiting for transfers between devices, local(): lax.psum_scatter(terms[2], 'fsdp', scatter_dimension=0, tiled=True)  67.3 us
    reduce_scatter x1, waiting for transfers between devices, local(): lax.psum_scatter(terms[0], 'fsdp', scatter_dimension=0, tiled=True)  60.3 us
    unnamed x4, blocking collectives  48.9 us
    all_to_all x1, blocking collectives, local(): lax.all_to_all(grads_outgoing, 'seq', split_axis=1, concat_axis=3, tiled=...  28.2 us
    all_gather x1, waiting for transfers between devices, local(): lax.all_gather(down_weight, 'fsdp', axis=1, tiled=True)  24.5 us
    all_gather x1, blocking collectives, local(): lax.all_gather(parts[2].astype(jnp.bfloat16), 'seq', axis=0, tiled=True)  17.3 us
    reduce_scatter x1, waiting for transfers between devices, local(): lax.psum_scatter(terms[3], 'fsdp', scatter_dimension=1, tiled=True)  17.1 us
    all_to_all x1, waiting for transfers between devices, local(): lax.all_to_all(packed, 'seq', split_axis=3, concat_axis=1, tiled=True)  15.7 us
  transfers between devices with their start and end apart: 14, of which 9 were waited for; matrix products, arithmetic and copies ran while one was open for 18% of the time, Pallas kernels for 0%

commit v1 on v0

v1 whole, which is shorter than its diff:
```python
import functools

import jax
import jax.numpy as jnp
from jax import lax
from jax.experimental import pallas as pl
from jax.experimental.pallas import tpu as pltpu
from jax.sharding import PartitionSpec as P

HEADS = 12
HEAD_DIM = 64
MESH = pl.DeviceIdType.MESH

eps = 1e-05
theta = 160000.0


def exchange_kernel(kinds, seq_n, fsdp_n, *refs):
    count = len(kinds)
    ins = refs[:count]
    outs = refs[count : 2 * count]
    rest = list(refs[2 * count :])
    z = lax.axis_index("seq")
    f = lax.axis_index("fsdp")
    pairs = fsdp_n // 2
    chip = f // 2
    core = f % 2
    partner = chip * 2 + 1 - core
    on_seq = any(kind in ("gather", "swap") for kind in kinds)
    on_fsdp = any(kind in ("spread", "reduce") for kind in kinds)

    barrier = pltpu.get_barrier_semaphore()
    waits = 0
    if on_seq:
        for d in range(1, seq_n):
            pl.semaphore_signal(
                barrier, inc=1, device_id={"seq": (z + d) % seq_n}, device_id_type=MESH
            )
        waits += seq_n - 1
    if on_fsdp:
        for d in range(1, pairs):
            pl.semaphore_signal(
                barrier,
                inc=1,
                device_id={"fsdp": ((chip + d) % pairs) * 2 + core},
                device_id_type=MESH,
            )
        pl.semaphore_signal(barrier, inc=1, device_id={"fsdp": partner}, device_id_type=MESH)
        waits += pairs
    pl.semaphore_wait(barrier, waits)

    def remote(src, dst, send, recv, where):
        return pltpu.make_async_remote_copy(
            src_ref=src,
            dst_ref=dst,
            send_sem=send,
            recv_sem=recv,
            device_id=where,
            device_id_type=MESH,
        )

    work = []
    for kind, src, dst in zip(kinds, ins, outs):
        extra = [rest.pop(0) for _ in range({"gather": 3, "swap": 3, "spread": 5, "reduce": 6}[kind])]
        work.append((kind, src, dst, extra))
    finish = []

    for kind, src, dst, extra in work:
        if kind == "reduce":
            held, total, send_a, recv_a, send_b, recv_b = extra
            for d in range(pairs):
                block = ((chip + d) % pairs) * 2
                remote(
                    src.at[block + 1 - core], held.at[d], send_a.at[d], recv_a.at[d], {"fsdp": partner}
                ).start()
    for kind, src, dst, extra in work:
        if kind in ("gather", "swap"):
            send, recv, own = extra
            for d in range(1, seq_n):
                to = (z + d) % seq_n
                piece = src if kind == "gather" else src.at[to]
                copy = remote(piece, dst.at[z], send.at[d], recv.at[d], {"seq": to})
                copy.start()
                finish.append(copy.wait_send)
                origin = (z + seq_n - d) % seq_n
                arrival = remote(piece, dst.at[origin], send.at[d], recv.at[d], {"seq": to})
                finish.append(arrival.wait_recv)
            local_copy = pltpu.make_async_copy(
                src if kind == "gather" else src.at[z], dst.at[z], own.at[0]
            )
            local_copy.start()
            finish.append(local_copy.wait)
        elif kind == "spread":
            send_a, recv_a, send_b, recv_b, own = extra
            for d in range(1, pairs):
                copy = remote(
                    src,
                    dst.at[f],
                    send_a.at[d],
                    recv_a.at[d],
                    {"fsdp": ((chip + d) % pairs) * 2 + core},
                )
                copy.start()
                finish.append(copy.wait_send)
            copy = remote(src, dst.at[f], send_b.at[0], recv_b.at[0], {"fsdp": partner})
            copy.start()
            finish.append(copy.wait_send)
            local_copy = pltpu.make_async_copy(src, dst.at[f], own.at[0])
            local_copy.start()
            finish.append(local_copy.wait)
    for kind, src, dst, extra in work:
        if kind == "reduce":
            held, total, send_a, recv_a, send_b, recv_b = extra
            for d in list(range(1, pairs)) + [0]:
                block = ((chip + d) % pairs) * 2
                pair_copy = remote(
                    src.at[block + 1 - core], held.at[d], send_a.at[d], recv_a.at[d], {"fsdp": partner}
                )
                pair_copy.wait_recv()
                finish.append(pair_copy.wait_send)
                value = (
                    src[block + core].astype(jnp.float32) + held[d].astype(jnp.float32)
                ).astype(src.dtype)
                if d == 0:
                    dst[0] = value
                else:
                    total[d] = value
                    copy = remote(
                        total.at[d], dst.at[d], send_b.at[d], recv_b.at[d], {"fsdp": block + core}
                    )
                    copy.start()
                    finish.append(copy.wait)
    for d in range(1, pairs):
        for kind, src, dst, extra in work:
            if kind == "spread":
                send_a, recv_a, send_b, recv_b, own = extra
                origin = ((chip + pairs - d) % pairs) * 2 + core
                remote(src, dst.at[origin], send_a.at[d], recv_a.at[d], {"fsdp": partner}).wait_recv()
                copy = remote(
                    dst.at[origin], dst.at[origin], send_b.at[d], recv_b.at[d], {"fsdp": partner}
                )
                copy.start()
                finish.append(copy.wait_send)
    for kind, src, dst, extra in work:
        if kind == "spread":
            send_a, recv_a, send_b, recv_b, own = extra
            for d in range(pairs):
                origin = ((chip + pairs - d) % pairs) * 2 + 1 - core
                finish.append(
                    remote(
                        src, dst.at[origin], send_b.at[d], recv_b.at[d], {"fsdp": partner}
                    ).wait_recv
                )
    for wait in finish:
        wait()


def exchange(kinds, arrays, collective_id):
    seq_n = lax.axis_size("seq")
    fsdp_n = lax.axis_size("fsdp")
    pairs = fsdp_n // 2
    shapes = []
    scratch = []
    dma = pltpu.SemaphoreType.DMA
    for kind, array in zip(kinds, arrays):
        if kind == "gather":
            shapes.append((seq_n,) + array.shape)
            scratch += [dma((seq_n,)), dma((seq_n,)), dma((1,))]
        elif kind == "swap":
            shapes.append(array.shape)
            scratch += [dma((seq_n,)), dma((seq_n,)), dma((1,))]
        elif kind == "spread":
            shapes.append((fsdp_n,) + array.shape)
            scratch += [dma((pairs,))] * 4 + [dma((1,))]
        else:
            shapes.append((pairs,) + array.shape[1:])
            scratch += [pltpu.VMEM((pairs,) + array.shape[1:], array.dtype)] * 2
            scratch += [dma((pairs,))] * 4
    space = pl.BlockSpec(memory_space=pltpu.VMEM)
    return pl.pallas_call(
        functools.partial(exchange_kernel, tuple(kinds), seq_n, fsdp_n),
        out_shape=[jax.ShapeDtypeStruct(s, a.dtype) for s, a in zip(shapes, arrays)],
        in_specs=[space] * len(kinds),
        out_specs=[space] * len(kinds),
        scratch_shapes=scratch,
        compiler_params=pltpu.CompilerParams(collective_id=collective_id, has_side_effects=True),
        name=f"exchange_{collective_id}",
    )(*arrays)


def layer_norm(values, gain_vec):
    middle = jnp.mean(values, axis=-1, keepdims=True)
    centred = values - middle
    inverse = lax.rsqrt(jnp.mean(centred * centred, axis=-1, keepdims=True) + eps)
    scaled = centred * inverse
    return (scaled * gain_vec, scaled, inverse)


def norm_back(upstream, scaled, inverse, gain_vec):
    weighted = upstream * gain_vec
    return inverse * (
        weighted
        - jnp.mean(weighted, axis=-1, keepdims=True)
        - scaled * jnp.mean(weighted * scaled, axis=-1, keepdims=True)
    )


def rotary_tables(positions, head_size):
    half_dim = head_size // 2
    frequency = theta ** (-jnp.arange(half_dim, dtype=jnp.float32) / half_dim)
    angles = positions.astype(jnp.float32)[..., None] * frequency
    return (jnp.cos(angles), jnp.sin(angles))


def rotate(values, cosine_table, sine_table):
    half_dim = values.shape[-1] // 2
    first_half = values[..., :half_dim]
    second_half = values[..., half_dim:]
    return jnp.concatenate(
        [
            first_half * cosine_table - second_half * sine_table,
            second_half * cosine_table + first_half * sine_table,
        ],
        axis=-1,
    )


def gelu_slope(values):
    return (
        0.5 * (1.0 + lax.erf(values * 0.7071067811865476))
        + values * jnp.exp(-0.5 * values * values) * 0.3989422804014327
    )


def dot(left, right, left_dim=1, right_dim=0):
    return lax.dot_general(
        left, right, (((left_dim,), (right_dim,)), ((), ())), preferred_element_type=jnp.float32
    )


def local(
    tokens,
    positions,
    norm1_gain,
    qkv_weight,
    out_weight,
    norm2_gain,
    in_weight,
    down_weight,
    cotangent,
):
    f32 = jnp.float32
    low = jnp.bfloat16
    groups = lax.axis_size("seq")
    fsdp_n = lax.axis_size("fsdp")
    z = lax.axis_index("seq")
    seq_dev, span_len, width = tokens.shape
    rows = seq_dev * span_len
    length = span_len * groups
    local_heads = HEADS // groups
    group_width = local_heads * HEAD_DIM
    shard = qkv_weight.shape[0]
    ff = down_weight.shape[0]
    ff_part = ff // groups
    scale = HEAD_DIM ** (-0.5)

    qkv_part = lax.dynamic_index_in_dim(
        qkv_weight.reshape(shard, 3, groups, group_width), z, 2, keepdims=False
    ).reshape(shard, 3 * group_width)
    in_part = lax.dynamic_index_in_dim(
        in_weight.reshape(shard, 2, groups, ff_part), z, 2, keepdims=False
    ).reshape(shard, 2 * ff_part)
    down_part = lax.dynamic_slice_in_dim(down_weight, z * ff_part, ff_part, 0).T
    gains = jnp.stack([norm1_gain, norm2_gain])
    own_tokens = tokens.reshape(rows, width)
    own_cotangent = cotangent.reshape(rows, width)

    def whole(stack):
        w = stack.shape[-1]
        return jnp.swapaxes(stack.reshape(groups, seq_dev, span_len, w), 0, 1).reshape(
            seq_dev * length, w
        )

    def spans(full):
        w = full.shape[-1]
        return jnp.swapaxes(full.reshape(seq_dev, groups, span_len, w), 0, 1).reshape(
            groups, rows, w
        )

    all_tokens, all_cot, all_pos, w_qkv, w_out, w_in, w_down, all_gains = exchange(
        ["gather", "gather", "gather", "spread", "spread", "spread", "spread", "spread"],
        [own_tokens, own_cotangent, positions, qkv_part, out_weight, in_part, down_part, gains],
        0,
    )
    all_tokens = whole(all_tokens)
    all_cot = whole(all_cot)
    all_pos = jnp.swapaxes(all_pos, 0, 1).reshape(seq_dev, length)
    w_qkv = w_qkv.reshape(width, 3 * group_width)
    w_out = w_out.reshape(width, width)
    w_in = w_in.reshape(width, 2 * ff_part)
    w_down = w_down.reshape(width, ff_part)
    gain_one = all_gains[:, 0].reshape(width).astype(f32)
    gain_two = all_gains[:, 1].reshape(width).astype(f32)

    normed_one, scaled_full, _ = layer_norm(all_tokens.astype(f32), gain_one)
    normed_one = normed_one.astype(low)
    projected = dot(normed_one, w_qkv).reshape(seq_dev, length, 3, local_heads, HEAD_DIM)
    projected = projected.transpose(2, 0, 3, 1, 4)
    cosine, sine = rotary_tables(all_pos, HEAD_DIM)
    cosine = cosine[:, None]
    sine = sine[:, None]
    query = rotate(projected[0], cosine, sine).astype(low)
    key = rotate(projected[1], cosine, sine).astype(low)
    value = projected[2].astype(low)
    scores = jnp.einsum("bhqd,bhkd->bhqk", query, key, preferred_element_type=f32) * scale
    totals = jax.nn.logsumexp(scores, axis=-1, keepdims=True)
    probs = jnp.exp(scores - totals)
    probs_low = probs.astype(low)
    attended = jnp.einsum("bhqk,bhkd->bhqd", probs_low, value, preferred_element_type=f32).astype(
        low
    )

    def to_rows(heads):
        return heads.transpose(0, 2, 1, 3).reshape(seq_dev * length, group_width)

    (mixed,) = exchange(["swap"], [spans(to_rows(attended))], 1)
    mixed = jnp.swapaxes(mixed, 0, 1).reshape(rows, width)
    inputs = own_tokens.astype(f32)
    residual = inputs + dot(mixed, w_out)
    normed_two, scaled_two, inverse_two = layer_norm(residual, gain_two)
    normed_two = normed_two.astype(low)
    (normed_full,) = exchange(["gather"], [normed_two], 2)
    normed_full = whole(normed_full)
    lifted = dot(normed_full, w_in)
    act = lifted[:, :ff_part]
    gate = lifted[:, ff_part:]
    activated = jax.nn.gelu(act, approximate=False)
    gated = (activated * gate).astype(low)
    gated_grad = dot(all_cot, w_down)
    lifted_grad = jnp.concatenate(
        [gated_grad * gate * gelu_slope(act), gated_grad * activated], axis=1
    ).astype(low)
    ffn_part = dot(gated, w_down, 1, 1).astype(low)
    normed_grad_part = dot(lifted_grad, w_in, 1, 1).astype(low)
    ffn_parts, normed_grad_parts = exchange(
        ["swap", "swap"], [spans(ffn_part), spans(normed_grad_part)], 3
    )
    block_out = (residual + jnp.sum(ffn_parts.astype(f32), axis=0)).astype(low)
    normed_two_grad = jnp.sum(normed_grad_parts.astype(f32), axis=0)
    gain_two_grad = jnp.sum(normed_two_grad * scaled_two, axis=0)
    residual_grad = own_cotangent.astype(f32) + norm_back(
        normed_two_grad, scaled_two, inverse_two, gain_two
    )
    residual_low = residual_grad.astype(low)
    mixed_grad = dot(residual_low, w_out, 1, 1).astype(low)
    (head_grad,) = exchange(
        ["swap"], [jnp.swapaxes(mixed_grad.reshape(rows, groups, group_width), 0, 1)], 4
    )
    head_grad = whole(head_grad).reshape(seq_dev, length, local_heads, HEAD_DIM)
    head_grad = head_grad.transpose(0, 2, 1, 3)
    delta = jnp.sum(head_grad.astype(f32) * attended.astype(f32), axis=-1, keepdims=True)
    value_grad = jnp.einsum("bhqk,bhqd->bhkd", probs_low, head_grad, preferred_element_type=f32)
    prob_grad = jnp.einsum("bhqd,bhkd->bhqk", head_grad, value, preferred_element_type=f32)
    score_grad = (probs * (prob_grad - delta)).astype(low)
    query_grad = jnp.einsum("bhqk,bhkd->bhqd", score_grad, key, preferred_element_type=f32) * scale
    key_grad = jnp.einsum("bhqk,bhqd->bhkd", score_grad, query, preferred_element_type=f32) * scale
    qkv_grad = jnp.concatenate(
        [
            to_rows(rotate(query_grad.astype(low).astype(f32), cosine, -sine).astype(low)),
            to_rows(rotate(key_grad.astype(low).astype(f32), cosine, -sine).astype(low)),
            to_rows(value_grad.astype(low)),
        ],
        axis=1,
    )
    normed_one_grad_part = dot(qkv_grad, w_qkv, 1, 1)
    gain_one_grad = jnp.sum(normed_one_grad_part * scaled_full, axis=0)

    qkv_term = dot(normed_one, qkv_grad, 0, 0).astype(low)
    in_term = dot(normed_full, lifted_grad, 0, 0).astype(low)
    down_term = dot(all_cot, gated, 0, 0).astype(low)
    out_term = dot(mixed, residual_low, 0, 0).astype(low)
    gain_terms = jnp.stack(
        [gain_one_grad.reshape(fsdp_n, shard), gain_two_grad.reshape(fsdp_n, shard)], axis=1
    )
    parts = exchange(
        ["swap", "reduce", "reduce", "reduce", "reduce", "reduce"],
        [spans(normed_one_grad_part.astype(low))]
        + [t.reshape(fsdp_n, shard, t.shape[1]) for t in (qkv_term, in_term, down_term, out_term)]
        + [gain_terms],
        5,
    )
    normed_one_grad = jnp.sum(parts[0].astype(f32), axis=0)
    _, scaled_one, inverse_one = layer_norm(inputs, gain_one)
    input_grad = (
        residual_grad + norm_back(normed_one_grad, scaled_one, inverse_one, gain_one)
    ).astype(low)
    owned = [jnp.sum(p.astype(f32), axis=0).astype(p.dtype) for p in parts[1:]]
    qkv_all, in_all, down_all, out_all, gain_all = exchange(["gather"] * 5, owned, 6)
    qkv_out = (
        qkv_all.reshape(groups, shard, 3, group_width)
        .transpose(1, 2, 0, 3)
        .reshape(shard, 3 * width)
        .astype(f32)
    )
    in_out = (
        in_all.reshape(groups, shard, 2, ff_part)
        .transpose(1, 2, 0, 3)
        .reshape(shard, 2 * ff)
        .astype(f32)
    )
    down_out = down_all.transpose(0, 2, 1).reshape(ff, shard).astype(f32)
    out_out = jnp.sum(out_all.astype(f32), axis=0)
    gain_out = jnp.sum(gain_all, axis=0)
    return (
        block_out.reshape(seq_dev, span_len, width),
        input_grad.reshape(seq_dev, span_len, width),
        qkv_out,
        out_out,
        in_out,
        down_out,
        gain_out[0],
        gain_out[1],
    )


def solution(mesh):
    in_specs = (
        P("fsdp", "seq", None),
        P("fsdp", "seq"),
        P("fsdp"),
        P("fsdp", None),
        P("fsdp", None),
        P("fsdp"),
        P("fsdp", None),
        P(None, "fsdp"),
        P("fsdp", "seq", None),
    )
    out_specs = (
        P("fsdp", "seq", None),
        P("fsdp", "seq", None),
        P("fsdp", None),
        P("fsdp", None),
        P("fsdp", None),
        P(None, "fsdp"),
        P("fsdp"),
        P("fsdp"),
    )
    return jax.shard_map(local, mesh=mesh, in_specs=in_specs, out_specs=out_specs, check_vma=False)
```

time: 491 us -> 280 us (0.57)
  waiting for transfers between devices: 212 us -> 0 us
  Pallas kernels: 0 us -> 199 us
  blocking collectives: 151 us -> 0 us
  matrix products: 43 us -> 23.8 us
  between operations: 17.3 us -> 1.5 us
  other arithmetic: 27.2 us -> 17.3 us
  starting transfers between devices: 8.59 us -> 0 us
  local copies, waits for them, and re-layouts: 30.4 us -> 36.8 us
    pallas_call x0 -> x7, Pallas kernels: none -> 199 us  [exchange(): pl.pallas_call(functools.partial(exchange_kernel, tuple(kinds), seq_n, fs...]
    reduce_scatter x7 -> x0, waiting for transfers between devices: 147 us -> none  [the longest x1 67.3 us: local(): lax.psum_scatter(terms[2], 'fsdp', scatter_dimension=0, tiled=True)]
    all_gather x4 -> x0, blocking collectives: 61.7 us -> none  [the longest x1 17.3 us: local(): lax.all_gather(parts[2].astype(jnp.bfloat16), 'seq', axis=0, tiled=True)]
    unnamed x4 -> x0, blocking collectives: 48.9 us -> none
    all_to_all x2 -> x0, blocking collectives: 40.7 us -> none  [the longest x1 28.2 us: local(): lax.all_to_all(grads_outgoing, 'seq', split_axis=1, concat_axis=3, tiled=...]
    all_gather x4 -> x0, waiting for transfers between devices: 39.9 us -> none  [the longest x1 24.5 us: local(): lax.all_gather(down_weight, 'fsdp', axis=1, tiled=True)]
    all_to_all x2 -> x0, waiting for transfers between devices: 22.1 us -> none  [the longest x1 15.7 us: local(): lax.all_to_all(packed, 'seq', split_axis=3, concat_axis=1, tiled=True)]
    dot_general x18, matrix products: 43 us -> 23.8 us  [the longest x12 17.4 us: dot(): lax.dot_general(left, right, (((left_dim,), (right_dim,)), ((), ())), pre...]
  transfers between devices with their start and end apart: 14 -> 0, of which waited for: 9 -> 0; matrix products, arithmetic and copies ran while one was open for 18% -> 0% of each run, Pallas kernels for 0% -> 0%
where the time goes in v1:
time: 280 us; the launch traced here: 279 us
  Pallas kernels  199 us (71%)
  local copies, waits for them, and re-layouts  36.8 us (13%)
  matrix products  23.8 us (8%)
  other arithmetic  17.3 us (6%)
    pallas_call x7, Pallas kernels, exchange(): pl.pallas_call(functools.partial(exchange_kernel, tuple(kinds), seq_n, fs...  199 us
    dot_general x12, matrix products, dot(): lax.dot_general(left, right, (((left_dim,), (right_dim,)), ((), ())), pre...  17.4 us

profile of v1, /device:TPU:0, one launch (start us, length us, event | category | flops | bytes accessed | tf_op | source)
XLA Modules:
  0.0 278.7 jit_solution(1796331325230493445)
XLA Ops:
  0.7 1.7 reshape.592
  2.9 0.8 copy.56.refs_3_
  3.7 0.7 reshape.594
  4.4 1.1 dynamic-slice_reduce_fusion
  5.4 0.8 reshape.595.refs_5_
  6.2 0.7 dynamic-slice_bitcast_fusion.refs_6_
  7.5 45.5 %exchange_0.1 = (bf16[4,128,768]{2,1,0:T(8,128)(2,1)}, bf16[4,128,768]{2,1,0:T(8,128)(2,1)}, s32[4,1,128]{2,1,0:T(1,128)}, bf16[8,96,576]{2,1,0:T(8,128)(2,1)}, ...) custom-call(bf16[128,768]{1,0:T(8,128)(2,1)} %bitcast.150, ...), custom_call_target="tpu_custom_call" | custom-call | tf_op jit(solution)/shard_map/exchange_0/pallas_call | solution.py:180
  53.0 1.6 copy.57
  55.3 0.8 fusion.9
  56.2 1.0 fusion.56
  57.4 0.6 multiply_reduce_fusion
  58.7 1.3 convolution_convert_fusion.6
  60.0 1.7 reshape_transpose_reshape_reshape.3
  61.7 1.8 copy.60.refs_0_
  63.5 8.9 %exchange_1.1 = bf16[4,128,192]{2,1,0:T(8,128)(2,1)} custom-call(bf16[4,128,192]{2,1,0:T(8,128)(2,1)} %copy.60.refs_0_), custom_call_target="tpu_custom_call" | custom-call | tf_op jit(solution)/shard_map/exchange_1/pallas_call | solution.py:180
  72.4 1.8 copy.61
  74.1 2.9 %fusion.68 = (f32[128]{0:T(128)}, f32[128,768]{1,0:T(8,128)}) fusion(bf16[128,768]{0,1:T(8,128)(2,1)} %bitcast.168, bf16[768,768]{1,0:T(8,128)(2,1)} %bitcast.151, bf16[1,128,768]{2,1,0:T(8,128)(2,1)} %param.9), kind=kOutput, calls=%fused_computation.154 | convolution fusion | flops 151289728 | bytes 1966592 | tf_op jit(solution)/shard_map/dot_general | solution.py:236
  77.1 0.7 broadcast_multiply_fusion.6
  77.8 1.2 multiply_reduce_fusion.6
  79.0 1.8 multiply_convert_fusion.5.refs_0_
  80.8 16.4 %exchange_2.1 = bf16[4,128,768]{2,1,0:T(8,128)(2,1)} custom-call(bf16[128,768]{1,0:T(8,128)(2,1)} %multiply_convert_fusion.5.refs_0_), custom_call_target="tpu_custom_call" | custom-call | tf_op jit(solution)/shard_map/exchange_2/pallas_call | solution.py:180
  97.2 2.2 fusion.70
  99.5 2.0 multiply_convert_fusion.3
  101.6 0.7 copy-done.10
  102.3 1.5 convolution_convert_fusion.4
  103.8 1.7 convolution_convert_fusion.3
  105.5 38.2 %exchange_3.1 = (bf16[4,128,768]{2,1,0:T(8,128)(2,1)}, bf16[4,128,768]{2,1,0:T(8,128)(2,1)}) custom-call(bf16[4,128,768]{2,1,0:T(8,128)(2,1)} %bitcast.159, bf16[4,128,768]{2,1,0:T(8,128)(2,1)} %bitcast.180), custom_call_target="tpu_custom_call" | custom-call | tf_op jit(solution)/shard_map/exchange_3/pallas_call | solution.py:180
  143.8 1.8 convert_reduce_fusion.1
  145.9 0.7 multiply_add_fusion
  146.6 0.7 copy-done.3
  147.4 1.2 convolution_convert_fusion.8
  148.6 1.7 copy.62
  150.3 1.8 copy.63
  152.1 11.6 %exchange_4.1 = bf16[4,128,192]{2,1,0:T(8,128)(2,1)} custom-call(bf16[4,128,192]{2,1,0:T(8,128)(2,1)} %bitcast.171), custom_call_target="tpu_custom_call" | custom-call | tf_op jit(solution)/shard_map/exchange_4/pallas_call | solution.py:180
  163.7 1.8 copy.64
  165.5 1.7 reshape_reshape_transpose_reshape.3
  167.2 1.7 convolution_convert_fusion.7
  168.9 1.9 multiply_convert_fusion
  171.7 0.6 fusion.7
  172.5 0.9 copy-done.7
  173.8 1.9 multiply_reduce_fusion.1
  175.7 0.6 convolution_convert_fusion.2
  176.3 1.3 copy.69
  177.7 0.6 convolution_convert_fusion.1
  178.3 1.3 copy.70
  180.1 1.1 copy.71
  181.1 1.5 convolution_convert_fusion
  182.8 0.6 pad_maximum_fusion.14.refs_5_
  183.4 32.0 %exchange_5.1 = (bf16[4,128,768]{2,1,0:T(8,128)(2,1)}, bf16[4,96,576]{2,1,0:T(8,128)(2,1)}, bf16[4,96,576]{2,1,0:T(8,128)(2,1)}, bf16[4,96,288]{2,1,0:T(8,128)(2...) custom-call(bf16[4,128,768]{2,1,0:T(8,128)(2,1)} %bitcast.182, bf16[8,96,576]{2,1,0:T(8,128)(2,1)} %bitcast.156, ...), custom_call_target="tpu_custom_call" | custom-call | tf_op jit(solution)/shard_map/exchange_5/pallas_call | solution.py:180
  215.4 1.3 convert_reduce_fusion
  217.4 0.9 fusion.44
  218.2 0.7 reduce_sum.245.refs_0_
  219.0 0.7 reduce_sum.246.refs_1_
  219.7 0.7 reduce_sum.247.refs_2_
  220.4 0.8 reduce_sum.248.refs_3_
  221.7 46.8 %exchange_6.1 = (bf16[4,96,576]{2,1,0:T(8,128)(2,1)}, bf16[4,96,576]{2,1,0:T(8,128)(2,1)}, bf16[4,96,288]{2,1,0:T(8,128)(2,1)}, bf16[4,96,768]{2,1,0:T(8,128)(2,1)}, f32[4,2,96]{2,1,0:T(2,128)}) custom-call(bf16[96,576]{1,0:T(8,128)(2,1)} %reduce_sum.245.refs_0_, bf16[96,576]{1,0:T(8,128)(2,1)} %reduce_sum.246.refs_1_, bf16[96,288]{1,0:T(8,128)(2,1)} %reduce_sum.247.refs_2_, ...), custom_call_target="tpu_custom_call" | custom-call | tf_op jit(solution)/shard_map/exchange_6/pallas_call | solution.py:180
  268.5 1.3 copy.72
  269.8 1.1 copy.73
  270.9 1.7 reshape.618
  272.6 0.8 convert_reduce_fusion.4
  273.4 0.9 reshape.622
  274.3 0.8 copy.74
  275.1 1.6 reshape.619
  277.1 1.1 reshape.620
  (144 shorter events, 7.3 us)
Async XLA Ops:
  0.6 5.6 %copy-start = (bf16[1152,96]{0,1:T(8,128)(2,1)S(1)}, bf16[1152,96]{0,1:T(8,128)(2,1)}, u32[]{:S(2)}) copy-start(bf16[1152,96]{0,1:T(8,128)(2,1)} %param.16) | copy-start | bytes 663556
  0.6 3.1 %copy-start.32 = (bf16[96,2304]{1,0:T(8,128)(2,1)S(1)}, bf16[96,2304]{1,0:T(8,128)(2,1)}, u32[]{:S(2)}) copy-start(bf16[96,2304]{1,0:T(8,128)(2,1)} %param.15) | copy-start | bytes 1327108
  2.3 4.6 %copy-start.46 = (bf16[96]{0:T(256)(128)(2,1)S(1)}, bf16[96]{0:T(256)(128)(2,1)}, u32[]{:S(2)}) copy-start(bf16[96]{0:T(256)(128)(2,1)} %param.14) | copy-start | bytes 580
  2.3 4.6 %copy-start.47 = (bf16[96]{0:T(256)(128)(2,1)S(1)}, bf16[96]{0:T(256)(128)(2,1)}, u32[]{:S(2)}) copy-start(bf16[96]{0:T(256)(128)(2,1)} %param.11) | copy-start | bytes 580
  52.9 1.6 copy-start.36
  52.9 1.7 copy-start.6
  54.9 1.3 copy-start.41
  55.3 0.9 copy-start.43
  55.3 0.9 copy-start.45
  56.2 2.6 copy-start.12
  57.4 0.7 copy-start.17
  57.4 0.7 copy-start.19
  57.4 0.7 copy-start.21
  79.0 20.5 %copy-start.37 = (f32[128]{0:T(128)}, f32[128]{0:T(128)S(1)}, u32[]{:S(2)}) copy-start(f32[128]{0:T(128)S(1)} %add_rsqrt_fusion.1) | copy-start | bytes 1540
  97.2 2.3 copy-start.23
  97.2 2.3 copy-start.26
  101.4 2.4 copy-start.48
  101.5 2.3 copy-start.50
  101.5 2.3 copy-start.16
  101.6 0.7 copy-start.10
  143.8 1.8 copy-start.1
  143.8 1.8 copy-start.38
  143.8 2.1 copy-start.25
  145.6 1.8 copy-start.5
  146.6 0.7 copy-start.3
  167.1 1.7 copy-start.9
  167.1 1.7 copy-start.13
  168.9 1.9 copy-start.20
  168.9 1.9 copy-start.22
  170.8 0.9 copy-start.18
  171.2 1.1 copy-start.35
  172.3 1.1 copy-start.7
  172.3 1.4 copy-start.15
  172.3 1.4 copy-start.42
  172.4 1.4 copy-start.44
  176.3 1.4 copy-start.8
  176.3 1.3 copy-start.49
  176.3 1.4 copy-start.51
  178.3 1.4 copy-start.11
  178.3 1.4 copy-start.24
  179.7 1.5 copy-start.4
  179.7 1.5 copy-start.14
  183.4 33.4 %copy-start.2 = (bf16[1,128,768]{2,1,0:T(8,128)(2,1)S(1)}, bf16[1,128,768]{2,1,0:T(8,128)(2,1)}, u32[]{:S(2)}) copy-start(bf16[1,128,768]{2,1,0:T(8,128)(2,1)} %param.9) | copy-start | bytes 589828
  215.4 2.8 %copy-start.30 = (bf16[4,96,576]{2,1,0:T(8,128)(2,1)S(1)}, bf16[4,96,576]{2,1,0:T(8,128)(2,1)}, u32[]{:S(2)}) copy-start(bf16[4,96,576]{2,1,0:T(8,128)(2,1)} %get-tuple-element.40) | copy-start | bytes 1327108
  216.8 2.2 copy-start.29
  216.9 2.8 %copy-start.34 = (bf16[4,96,288]{2,1,0:T(8,128)(2,1)S(1)}, bf16[4,96,288]{2,1,0:T(8,128)(2,1)}, u32[]{:S(2)}) copy-start(bf16[4,96,288]{2,1,0:T(8,128)(2,1)} %get-tuple-element.42) | copy-start | bytes 663556
  217.1 3.3 %copy-start.27 = (bf16[4,96,768]{2,1,0:T(8,128)(2,1)S(1)}, bf16[4,96,768]{2,1,0:T(8,128)(2,1)}, u32[]{:S(2)}) copy-start(bf16[4,96,768]{2,1,0:T(8,128)(2,1)} %get-tuple-element.43) | copy-start | bytes 1769476
  217.3 3.8 %copy-start.39 = (f32[4,2,96]{2,1,0:T(2,128)S(1)}, f32[4,2,96]{2,1,0:T(2,128)}, u32[]{:S(2)}) copy-start(f32[4,2,96]{2,1,0:T(2,128)} %get-tuple-element.44) | copy-start | bytes 9220
  270.9 1.7 copy-start.28
  270.9 2.5 copy-start.31
  275.0 1.6 copy-start.33
  276.7 1.5 copy-start.40

commit v2 on v1

--- a/solution.py
+++ b/solution.py
@@ -15,7 +15,11 @@
 theta = 160000.0
 
 
+EXTRA = {"gather": 4, "swap": 3, "spread": 5, "fold": 8, "grad": 11}
+
+
 def exchange_kernel(kinds, seq_n, fsdp_n, *refs):
+    f32 = jnp.float32
     count = len(kinds)
     ins = refs[:count]
     outs = refs[count : 2 * count]
@@ -26,8 +30,8 @@
     chip = f // 2
     core = f % 2
     partner = chip * 2 + 1 - core
-    on_seq = any(kind in ("gather", "swap") for kind in kinds)
-    on_fsdp = any(kind in ("spread", "reduce") for kind in kinds)
+    on_seq = any(kind != "spread" for kind in kinds)
+    on_fsdp = any(kind in ("spread", "grad") for kind in kinds)
 
     barrier = pltpu.get_barrier_semaphore()
     waits = 0
@@ -59,127 +63,254 @@
             device_id_type=MESH,
         )
 
-    work = []
+    groups = {kind: [] for kind in EXTRA}
     for kind, src, dst in zip(kinds, ins, outs):
-        extra = [rest.pop(0) for _ in range({"gather": 3, "swap": 3, "spread": 5, "reduce": 6}[kind])]
-        work.append((kind, src, dst, extra))
+        groups[kind].append((src, dst, [rest.pop(0) for _ in range(EXTRA[kind])]))
     finish = []
-
-    for kind, src, dst, extra in work:
-        if kind == "reduce":
-            held, total, send_a, recv_a, send_b, recv_b = extra
-            for d in range(pairs):
-                block = ((chip + d) % pairs) * 2
-                remote(
-                    src.at[block + 1 - core], held.at[d], send_a.at[d], recv_a.at[d], {"fsdp": partner}
-                ).start()
-    for kind, src, dst, extra in work:
-        if kind in ("gather", "swap"):
-            send, recv, own = extra
-            for d in range(1, seq_n):
-                to = (z + d) % seq_n
-                piece = src if kind == "gather" else src.at[to]
-                copy = remote(piece, dst.at[z], send.at[d], recv.at[d], {"seq": to})
-                copy.start()
-                finish.append(copy.wait_send)
-                origin = (z + seq_n - d) % seq_n
-                arrival = remote(piece, dst.at[origin], send.at[d], recv.at[d], {"seq": to})
-                finish.append(arrival.wait_recv)
-            local_copy = pltpu.make_async_copy(
-                src if kind == "gather" else src.at[z], dst.at[z], own.at[0]
+    up = {"seq": lax.rem(z + 1, seq_n)}
+    down = {"seq": lax.rem(z + seq_n - 1, seq_n)}
+    has_up = z < seq_n - 1
+    has_down = z > 0
+
+    def line_start(dst, sems, src):
+        up_send, up_recv, down_send, down_recv = sems
+
+        @pl.when(has_up)
+        def _():
+            remote(src, dst.at[z], up_send.at[0], up_recv.at[1], up).start()
+
+        @pl.when(has_down)
+        def _():
+            remote(src, dst.at[z], down_send.at[0], down_recv.at[1], down).start()
+
+    def line_step(dst, sems, d):
+        up_send, up_recv, down_send, down_recv = sems
+
+        @pl.when(z >= d)
+        def _():
+            block = dst.at[lax.rem(z + seq_n - d, seq_n)]
+            remote(block, block, up_send.at[d], up_recv.at[d], up).wait_recv()
+            if d < seq_n - 1:
+
+                @pl.when(has_up)
+                def _():
+                    remote(block, block, up_send.at[d], up_recv.at[d + 1], up).start()
+
+        @pl.when(z + d < seq_n)
+        def _():
+            block = dst.at[lax.rem(z + d, seq_n)]
+            remote(block, block, down_send.at[d], down_recv.at[d], down).wait_recv()
+            if d < seq_n - 1:
+
+                @pl.when(has_down)
+                def _():
+                    remote(block, block, down_send.at[d], down_recv.at[d + 1], down).start()
+
+    def line_end(dst, sems, src):
+        up_send, up_recv, down_send, down_recv = sems
+        for d in range(seq_n - 1):
+
+            @pl.when(jnp.logical_and(has_up, z >= d))
+            def _():
+                block = src if d == 0 else dst.at[lax.rem(z + seq_n - d, seq_n)]
+                remote(block, dst.at[z], up_send.at[d], up_recv.at[d + 1], up).wait_send()
+
+            @pl.when(jnp.logical_and(has_down, z + d < seq_n))
+            def _():
+                block = src if d == 0 else dst.at[lax.rem(z + d, seq_n)]
+                remote(block, dst.at[z], down_send.at[d], down_recv.at[d + 1], down).wait_send()
+
+    for src, dst, extra in groups["grad"]:
+        held, total, send_a, recv_a, send_b, recv_b = extra[:6]
+        for d in range(pairs):
+            block = ((chip + d) % pairs) * 2
+            remote(
+                src.at[block + 1 - core], held.at[d], send_a.at[d], recv_a.at[d], {"fsdp": partner}
+            ).start()
+    for src, dst, extra in groups["fold"]:
+        up_buf, up_sum, down_buf, down_sum, up_send, up_recv, down_send, down_recv = extra
+        for k in range(seq_n - 1):
+            t = seq_n - 1 - k
+
+            @pl.when(z == 0)
+            def _():
+                remote(src.at[t], up_buf.at[t], up_send.at[t], up_recv.at[t], up).start()
+
+            @pl.when(z == seq_n - 1)
+            def _():
+                remote(src.at[k], down_buf.at[k], down_send.at[k], down_recv.at[k], down).start()
+
+    for src, dst, extra in groups["gather"]:
+        line_start(dst, extra, src)
+    for src, dst, extra in groups["swap"]:
+        send, recv, own = extra
+        for d in range(1, seq_n):
+            to = (z + d) % seq_n
+            piece = src.at[to]
+            copy = remote(piece, dst.at[z], send.at[d], recv.at[d], {"seq": to})
+            copy.start()
+            finish.append(copy.wait_send)
+            origin = (z + seq_n - d) % seq_n
+            arrival = remote(piece, dst.at[origin], send.at[d], recv.at[d], {"seq": to})
+            finish.append(arrival.wait_recv)
+        local_copy = pltpu.make_async_copy(src.at[z], dst.at[z], own.at[0])
+        local_copy.start()
+        finish.append(local_copy.wait)
+    for src, dst, extra in groups["spread"]:
+        send_a, recv_a, send_b, recv_b, own = extra
+        for d in range(1, pairs):
+            copy = remote(
+                src,
+                dst.at[f],
+                send_a.at[d],
+                recv_a.at[d],
+                {"fsdp": ((chip + d) % pairs) * 2 + core},
             )
-            local_copy.start()
-            finish.append(local_copy.wait)
-        elif kind == "spread":
-            send_a, recv_a, send_b, recv_b, own = extra
-            for d in range(1, pairs):
+            copy.start()
+            finish.append(copy.wait_send)
+        copy = remote(src, dst.at[f], send_b.at[0], recv_b.at[0], {"fsdp": partner})
+        copy.start()
+        finish.append(copy.wait_send)
+        local_copy = pltpu.make_async_copy(src, dst.at[f], own.at[0])
+        local_copy.start()
+        finish.append(local_copy.wait)
+    for src, dst, extra in groups["gather"]:
+        dst[z] = src[...]
+    for src, dst, extra in groups["grad"]:
+        held, total, send_a, recv_a, send_b, recv_b = extra[:6]
+        for d in list(range(1, pairs)) + [0]:
+            block = ((chip + d) % pairs) * 2
+            pair_copy = remote(
+                src.at[block + 1 - core], held.at[d], send_a.at[d], recv_a.at[d], {"fsdp": partner}
+            )
+            pair_copy.wait_recv()
+            finish.append(pair_copy.wait_send)
+            total[d] = (src[block + core].astype(f32) + held[d].astype(f32)).astype(src.dtype)
+            if d > 0:
                 copy = remote(
-                    src,
-                    dst.at[f],
-                    send_a.at[d],
-                    recv_a.at[d],
-                    {"fsdp": ((chip + d) % pairs) * 2 + core},
+                    total.at[d],
+                    extra[10].at[d],
+                    send_b.at[d],
+                    recv_b.at[d],
+                    {"fsdp": block + core},
                 )
                 copy.start()
                 finish.append(copy.wait_send)
-            copy = remote(src, dst.at[f], send_b.at[0], recv_b.at[0], {"fsdp": partner})
-            copy.start()
-            finish.append(copy.wait_send)
-            local_copy = pltpu.make_async_copy(src, dst.at[f], own.at[0])
-            local_copy.start()
-            finish.append(local_copy.wait)
-    for kind, src, dst, extra in work:
-        if kind == "reduce":
-            held, total, send_a, recv_a, send_b, recv_b = extra
-            for d in list(range(1, pairs)) + [0]:
-                block = ((chip + d) % pairs) * 2
-                pair_copy = remote(
-                    src.at[block + 1 - core], held.at[d], send_a.at[d], recv_a.at[d], {"fsdp": partner}
-                )
-                pair_copy.wait_recv()
-                finish.append(pair_copy.wait_send)
-                value = (
-                    src[block + core].astype(jnp.float32) + held[d].astype(jnp.float32)
-                ).astype(src.dtype)
-                if d == 0:
-                    dst[0] = value
-                else:
-                    total[d] = value
-                    copy = remote(
-                        total.at[d], dst.at[d], send_b.at[d], recv_b.at[d], {"fsdp": block + core}
-                    )
-                    copy.start()
-                    finish.append(copy.wait)
-    for d in range(1, pairs):
-        for kind, src, dst, extra in work:
-            if kind == "spread":
-                send_a, recv_a, send_b, recv_b, own = extra
-                origin = ((chip + pairs - d) % pairs) * 2 + core
-                remote(src, dst.at[origin], send_a.at[d], recv_a.at[d], {"fsdp": partner}).wait_recv()
+    for d in range(1, seq_n):
+        for src, dst, extra in groups["gather"]:
+            line_step(dst, extra, d)
+        for src, dst, extra in groups["spread"]:
+            send_a, recv_a, send_b, recv_b, own = extra
+            for e in range(1, pairs):
+                if e % (seq_n - 1) != d % (seq_n - 1):
+                    continue
+                origin = ((chip + pairs - e) % pairs) * 2 + core
+                remote(src, dst.at[origin], send_a.at[e], recv_a.at[e], {"fsdp": partner}).wait_recv()
                 copy = remote(
-                    dst.at[origin], dst.at[origin], send_b.at[d], recv_b.at[d], {"fsdp": partner}
+                    dst.at[origin], dst.at[origin], send_b.at[e], recv_b.at[e], {"fsdp": partner}
                 )
                 copy.start()
                 finish.append(copy.wait_send)
-    for kind, src, dst, extra in work:
-        if kind == "spread":
-            send_a, recv_a, send_b, recv_b, own = extra
-            for d in range(pairs):
-                origin = ((chip + pairs - d) % pairs) * 2 + 1 - core
-                finish.append(
-                    remote(
-                        src, dst.at[origin], send_b.at[d], recv_b.at[d], {"fsdp": partner}
-                    ).wait_recv
-                )
+        k = d - 1
+        t = seq_n - 1 - k
+        for src, dst, extra in groups["fold"]:
+            up_buf, up_sum, down_buf, down_sum, up_send, up_recv, down_send, down_recv = extra
+
+            @pl.when(jnp.logical_and(z > 0, z < t))
+            def _():
+                remote(src.at[t], up_buf.at[t], up_send.at[t], up_recv.at[t], up).wait_recv()
+                up_sum[t] = (src[t].astype(f32) + up_buf[t].astype(f32)).astype(src.dtype)
+                remote(up_sum.at[t], up_buf.at[t], up_send.at[t], up_recv.at[t], up).start()
+
+            @pl.when(jnp.logical_and(z < seq_n - 1, z > k))
+            def _():
+                remote(src.at[k], down_buf.at[k], down_send.at[k], down_recv.at[k], down).wait_recv()
+                down_sum[k] = (src[k].astype(f32) + down_buf[k].astype(f32)).astype(src.dtype)
+                remote(down_sum.at[k], down_buf.at[k], down_send.at[k], down_recv.at[k], down).start()
+
+    for src, dst, extra in groups["grad"]:
+        held, total, send_a, recv_a, send_b, recv_b = extra[:6]
+        value = total[0].astype(f32)
+        for d in range(1, pairs):
+            remote(
+                total.at[d], extra[10].at[d], send_b.at[d], recv_b.at[d], {"fsdp": partner}
+            ).wait_recv()
+            value = value + extra[10][d].astype(f32)
+        dst[z] = value.astype(src.dtype)
+        line_start(dst, extra[6:10], dst.at[z])
+    for d in range(1, seq_n):
+        for src, dst, extra in groups["grad"]:
+            line_step(dst, extra[6:10], d)
+    for src, dst, extra in groups["fold"]:
+        up_buf, up_sum, down_buf, down_sum, up_send, up_recv, down_send, down_recv = extra
+        dst[...] = src[z].astype(f32)
+
+        @pl.when(z > 0)
+        def _():
+            remote(src.at[z], up_buf.at[z], up_send.at[z], up_recv.at[z], up).wait_recv()
+            dst[...] += up_buf[z].astype(f32)
+
+        @pl.when(z < seq_n - 1)
+        def _():
+            remote(src.at[z], down_buf.at[z], down_send.at[z], down_recv.at[z], down).wait_recv()
+            dst[...] += down_buf[z].astype(f32)
+
+        for t in range(seq_n):
+
+            @pl.when(z < t)
+            def _():
+                remote(src.at[t], up_buf.at[t], up_send.at[t], up_recv.at[t], up).wait_send()
+
+            @pl.when(z > t)
+            def _():
+                remote(src.at[t], down_buf.at[t], down_send.at[t], down_recv.at[t], down).wait_send()
+
+    for src, dst, extra in groups["spread"]:
+        send_a, recv_a, send_b, recv_b, own = extra
+        for d in range(pairs):
+            origin = ((chip + pairs - d) % pairs) * 2 + 1 - core
+            finish.append(
+                remote(src, dst.at[origin], send_b.at[d], recv_b.at[d], {"fsdp": partner}).wait_recv
+            )
     for wait in finish:
         wait()
+    for src, dst, extra in groups["gather"]:
+        line_end(dst, extra, src)
+    for src, dst, extra in groups["grad"]:
+        line_end(dst, extra[6:10], dst.at[z])
 
 
 def exchange(kinds, arrays, collective_id):
     seq_n = lax.axis_size("seq")
     fsdp_n = lax.axis_size("fsdp")
     pairs = fsdp_n // 2
-    shapes = []
+    results = []
     scratch = []
     dma = pltpu.SemaphoreType.DMA
     for kind, array in zip(kinds, arrays):
+        dtype = array.dtype
         if kind == "gather":
-            shapes.append((seq_n,) + array.shape)
+            shape = (seq_n,) + array.shape
+            scratch += [dma((seq_n,))] * 4
+        elif kind == "swap":
+            shape = array.shape
             scratch += [dma((seq_n,)), dma((seq_n,)), dma((1,))]
-        elif kind == "swap":
-            shapes.append(array.shape)
-            scratch += [dma((seq_n,)), dma((seq_n,)), dma((1,))]
+        elif kind == "fold":
+            shape = array.shape[1:]
+            scratch += [pltpu.VMEM(array.shape, dtype)] * 4 + [dma((seq_n,))] * 4
+            dtype = jnp.float32
         elif kind == "spread":
-            shapes.append((fsdp_n,) + array.shape)
+            shape = (fsdp_n,) + array.shape
             scratch += [dma((pairs,))] * 4 + [dma((1,))]
         else:
-            shapes.append((pairs,) + array.shape[1:])
-            scratch += [pltpu.VMEM((pairs,) + array.shape[1:], array.dtype)] * 2
-            scratch += [dma((pairs,))] * 4
+            shape = (seq_n,) + array.shape[1:]
+            half = pltpu.VMEM((pairs,) + array.shape[1:], dtype)
+            scratch += [half] * 2 + [dma((pairs,))] * 4 + [dma((seq_n,))] * 4 + [half]
+        results.append(jax.ShapeDtypeStruct(shape, dtype))
     space = pl.BlockSpec(memory_space=pltpu.VMEM)
     return pl.pallas_call(
         functools.partial(exchange_kernel, tuple(kinds), seq_n, fsdp_n),
-        out_shape=[jax.ShapeDtypeStruct(s, a.dtype) for s, a in zip(shapes, arrays)],
+        out_shape=results,
         in_specs=[space] * len(kinds),
         out_specs=[space] * len(kinds),
         scratch_shapes=scratch,
@@ -343,10 +474,10 @@
     ffn_part = dot(gated, w_down, 1, 1).astype(low)
     normed_grad_part = dot(lifted_grad, w_in, 1, 1).astype(low)
     ffn_parts, normed_grad_parts = exchange(
-        ["swap", "swap"], [spans(ffn_part), spans(normed_grad_part)], 3
-    )
-    block_out = (residual + jnp.sum(ffn_parts.astype(f32), axis=0)).astype(low)
-    normed_two_grad = jnp.sum(normed_grad_parts.astype(f32), axis=0)
+        ["fold", "fold"], [spans(ffn_part), spans(normed_grad_part)], 3
+    )
+    block_out = (residual + ffn_parts).astype(low)
+    normed_two_grad = normed_grad_parts
     gain_two_grad = jnp.sum(normed_two_grad * scaled_two, axis=0)
     residual_grad = own_cotangent.astype(f32) + norm_back(
         normed_two_grad, scaled_two, inverse_two, gain_two
@@ -383,19 +514,18 @@
         [gain_one_grad.reshape(fsdp_n, shard), gain_two_grad.reshape(fsdp_n, shard)], axis=1
     )
     parts = exchange(
-        ["swap", "reduce", "reduce", "reduce", "reduce", "reduce"],
+        ["fold", "grad", "grad", "grad", "grad", "grad"],
         [spans(normed_one_grad_part.astype(low))]
         + [t.reshape(fsdp_n, shard, t.shape[1]) for t in (qkv_term, in_term, down_term, out_term)]
         + [gain_terms],
         5,
     )
-    normed_one_grad = jnp.sum(parts[0].astype(f32), axis=0)
+    normed_one_grad = parts[0]
     _, scaled_one, inverse_one = layer_norm(inputs, gain_one)
     input_grad = (
         residual_grad + norm_back(normed_one_grad, scaled_one, inverse_one, gain_one)
     ).astype(low)
-    owned = [jnp.sum(p.astype(f32), axis=0).astype(p.dtype) for p in parts[1:]]
-    qkv_all, in_all, down_all, out_all, gain_all = exchange(["gather"] * 5, owned, 6)
+    qkv_all, in_all, down_all, out_all, gain_all = parts[1:]
     qkv_out = (
         qkv_all.reshape(groups, shard, 3, group_width)
         .transpose(1, 2, 0, 3)

time: 280 us -> 257 us (0.918)
  Pallas kernels: 199 us -> 180 us
    pallas_call x7 -> x6, Pallas kernels: 199 us -> 180 us  [exchange(): pl.pallas_call(functools.partial(exchange_kernel, tuple(kinds), seq_n, fs...]
    reduce_sum x7 -> x0, other arithmetic: 6.61 us -> none  [the longest x5 3.5 us: local(): owned = [jnp.sum(p.astype(f32), axis=0).astype(p.dtype) for p in parts[1:]]]
where the time goes in v2:
time: 257 us; the launch traced here: 256 us
  Pallas kernels  180 us (70%)
  local copies, waits for them, and re-layouts  35.4 us (14%)
  matrix products  23.8 us (9%)
  other arithmetic  15.2 us (6%)
    pallas_call x6, Pallas kernels, exchange(): pl.pallas_call(functools.partial(exchange_kernel, tuple(kinds), seq_n, fs...  180 us
    dot_general x12, matrix products, dot(): lax.dot_general(left, right, (((left_dim,), (right_dim,)), ((), ())), pre...  17.4 us

profile of v2, /device:TPU:0, one launch (start us, length us, event | category | flops | bytes accessed | tf_op | source)
XLA Modules:
  0.0 256.3 jit_solution(15820256526012750259)
XLA Ops:
  0.7 1.7 reshape.592
  2.9 0.8 copy.56.refs_3_
  3.7 0.7 reshape.594
  4.4 1.1 dynamic-slice_reduce_fusion
  5.4 0.8 reshape.595.refs_5_
  6.2 0.7 dynamic-slice_bitcast_fusion.refs_6_
  7.0 0.5 pad_maximum_fusion.15.refs_7_
  7.5 43.3 %exchange_0.1 = (bf16[4,128,768]{2,1,0:T(8,128)(2,1)}, bf16[4,128,768]{2,1,0:T(8,128)(2,1)}, s32[4,1,128]{2,1,0:T(1,128)}, bf16[8,96,576]{2,1,0:T(8,128)(2,1)}, ...) custom-call(bf16[128,768]{1,0:T(8,128)(2,1)} %bitcast.150, ...), custom_call_target="tpu_custom_call" | custom-call | tf_op jit(solution)/shard_map/exchange_0/pallas_call | solution.py:311
  50.8 1.6 copy.57
  53.1 0.8 fusion.9
  54.1 1.0 fusion.56
  55.3 0.6 multiply_reduce_fusion
  55.9 0.5 exponential_reduce_fusion
  56.5 1.3 convolution_convert_fusion.6
  57.8 1.7 reshape_transpose_reshape_reshape.3
  59.5 1.8 copy.60.refs_0_
  61.3 10.4 %exchange_1.1 = bf16[4,128,192]{2,1,0:T(8,128)(2,1)} custom-call(bf16[4,128,192]{2,1,0:T(8,128)(2,1)} %copy.60.refs_0_), custom_call_target="tpu_custom_call" | custom-call | tf_op jit(solution)/shard_map/exchange_1/pallas_call | solution.py:311
  71.7 1.8 copy.61
  73.5 2.9 %fusion.68 = (f32[128]{0:T(128)}, f32[128,768]{1,0:T(8,128)}) fusion(bf16[128,768]{0,1:T(8,128)(2,1)} %bitcast.168, bf16[768,768]{1,0:T(8,128)(2,1)} %bitcast.151, bf16[1,128,768]{2,1,0:T(8,128)(2,1)} %param.9), kind=kOutput, calls=%fused_computation.151 | convolution fusion | flops 151289728 | bytes 1966592 | tf_op jit(solution)/shard_map/dot_general | solution.py:367
  76.5 0.7 broadcast_multiply_fusion.6
  77.1 1.2 multiply_reduce_fusion.6
  78.3 1.8 multiply_convert_fusion.5.refs_0_
  80.1 18.4 %exchange_2.1 = bf16[4,128,768]{2,1,0:T(8,128)(2,1)} custom-call(bf16[128,768]{1,0:T(8,128)(2,1)} %multiply_convert_fusion.5.refs_0_), custom_call_target="tpu_custom_call" | custom-call | tf_op jit(solution)/shard_map/exchange_2/pallas_call | solution.py:311
  98.5 2.2 fusion.70
  100.8 2.0 multiply_convert_fusion.3
  102.9 0.7 copy-done.9
  103.6 1.5 convolution_convert_fusion.4
  105.1 1.7 convolution_convert_fusion.3
  106.8 40.2 %exchange_3.1 = (f32[128,768]{1,0:T(8,128)}, f32[128,768]{1,0:T(8,128)}) custom-call(bf16[4,128,768]{2,1,0:T(8,128)(2,1)} %bitcast.159, bf16[4,128,768]{2,1,0:T(8,128)(2,1)} %bitcast.180), custom_call_target="tpu_custom_call" | custom-call | tf_op jit(solution)/shard_map/exchange_3/pallas_call | solution.py:311
  147.0 1.4 multiply_reduce_fusion.3
  148.5 2.1 multiply_add_fusion
  150.5 0.7 copy-done.2
  151.3 1.2 convolution_convert_fusion.8
  152.5 1.7 copy.62
  154.2 1.8 copy.63
  156.0 9.1 %exchange_4.1 = bf16[4,128,192]{2,1,0:T(8,128)(2,1)} custom-call(bf16[4,128,192]{2,1,0:T(8,128)(2,1)} %bitcast.171), custom_call_target="tpu_custom_call" | custom-call | tf_op jit(solution)/shard_map/exchange_4/pallas_call | solution.py:311
  165.1 1.8 copy.64
  166.9 1.7 reshape_reshape_transpose_reshape.3
  168.6 1.7 convolution_convert_fusion.7
  170.4 1.9 multiply_convert_fusion
  172.7 0.5 copy-done.17
  173.2 0.6 fusion.7
  174.0 0.9 copy-done.6
  175.2 1.9 multiply_reduce_fusion.1
  177.1 0.6 convolution_convert_fusion.2
  177.8 1.3 copy.69
  179.1 0.6 convolution_convert_fusion.1
  179.8 1.3 copy.70
  181.1 0.4 convolution_convert_fusion.5
  181.5 1.1 copy.71
  182.6 1.5 convolution_convert_fusion
  184.2 0.6 pad_maximum_fusion.14.refs_5_
  184.8 59.2 %exchange_5.1 = (f32[128,768]{1,0:T(8,128)}, bf16[4,96,576]{2,1,0:T(8,128)(2,1)}, bf16[4,96,576]{2,1,0:T(8,128)(2,1)}, bf16[4,96,288]{2,1,0:T(8,128)(2,1)}, bf16...) custom-call(bf16[4,128,768]{2,1,0:T(8,128)(2,1)} %bitcast.182, bf16[8,96,576]{2,1,0:T(8,128)(2,1)} %bitcast.156, ...), custom_call_target="tpu_custom_call" | custom-call | tf_op jit(solution)/shard_map/exchange_5/pallas_call | solution.py:311
  244.4 1.2 multiply_reduce_fusion.7
  245.6 1.9 fusion.44
  247.7 0.8 copy.73
  248.6 1.7 reshape.618
  250.3 0.8 convert_reduce_fusion.1
  251.0 0.9 reshape.622
  251.9 0.8 copy.74
  252.7 1.6 reshape.619
  254.4 0.4 copy.75
  254.7 1.1 reshape.620
  255.8 0.5 slice_bitcast_fusion.2
  (121 shorter events, 3.5 us)
Async XLA Ops:
  0.6 5.6 %copy-start = (bf16[1152,96]{0,1:T(8,128)(2,1)S(1)}, bf16[1152,96]{0,1:T(8,128)(2,1)}, u32[]{:S(2)}) copy-start(bf16[1152,96]{0,1:T(8,128)(2,1)} %param.16) | copy-start | bytes 663556
  0.6 3.1 %copy-start.28 = (bf16[96,2304]{1,0:T(8,128)(2,1)S(1)}, bf16[96,2304]{1,0:T(8,128)(2,1)}, u32[]{:S(2)}) copy-start(bf16[96,2304]{1,0:T(8,128)(2,1)} %param.15) | copy-start | bytes 1327108
  2.3 4.6 %copy-start.39 = (bf16[96]{0:T(256)(128)(2,1)S(1)}, bf16[96]{0:T(256)(128)(2,1)}, u32[]{:S(2)}) copy-start(bf16[96]{0:T(256)(128)(2,1)} %param.14) | copy-start | bytes 580
  2.3 4.6 %copy-start.40 = (bf16[96]{0:T(256)(128)(2,1)S(1)}, bf16[96]{0:T(256)(128)(2,1)}, u32[]{:S(2)}) copy-start(bf16[96]{0:T(256)(128)(2,1)} %param.11) | copy-start | bytes 580
  50.8 1.6 copy-start.31
  50.8 1.7 copy-start.5
  52.7 1.3 copy-start.34
  53.1 0.9 copy-start.36
  53.1 0.9 copy-start.38
  54.0 2.5 copy-start.11
  55.2 0.7 copy-start.16
  55.2 0.7 copy-start.18
  55.3 0.7 copy-start.20
  78.3 22.4 %copy-start.32 = (f32[128]{0:T(128)}, f32[128]{0:T(128)S(1)}, u32[]{:S(2)}) copy-start(f32[128]{0:T(128)S(1)} %add_rsqrt_fusion.1) | copy-start | bytes 1540
  98.5 2.3 copy-start.22
  98.5 2.3 copy-start.24
  102.7 2.4 copy-start.41
  102.8 2.4 copy-start.43
  102.8 2.3 copy-start.15
  102.9 0.7 copy-start.9
  147.0 4.3 %copy-start.4 = (bf16[8,96,768]{2,1,0:T(8,128)(2,1)S(1)}, bf16[8,96,768]{2,1,0:T(8,128)(2,1)}, u32[]{:S(2)}) copy-start(bf16[8,96,768]{2,1,0:T(8,128)(2,1)} %get-tuple-element.28) | copy-start | bytes 3538948
  150.5 0.7 copy-start.2
  168.6 1.7 copy-start.8
  168.6 1.7 copy-start.12
  170.3 1.9 copy-start.19
  170.4 1.9 copy-start.21
  172.3 0.9 copy-start.17
  172.7 1.1 copy-start.30
  173.8 1.1 copy-start.6
  173.8 1.4 copy-start.14
  173.8 1.4 copy-start.35
  173.8 1.4 copy-start.37
  177.7 1.4 copy-start.7
  177.7 1.4 copy-start.42
  177.8 1.4 copy-start.44
  179.7 1.4 copy-start.10
  179.8 1.4 copy-start.23
  181.1 1.5 copy-start.3
  181.1 1.5 copy-start.13
  184.8 59.2 %copy-start.1 = (bf16[1,128,768]{2,1,0:T(8,128)(2,1)S(1)}, bf16[1,128,768]{2,1,0:T(8,128)(2,1)}, u32[]{:S(2)}) copy-start(bf16[1,128,768]{2,1,0:T(8,128)(2,1)} %param.9) | copy-start | bytes 589828
  244.0 3.5 %copy-start.27 = (bf16[4,96,576]{2,1,0:T(8,128)(2,1)S(1)}, bf16[4,96,576]{2,1,0:T(8,128)(2,1)}, u32[]{:S(2)}) copy-start(bf16[4,96,576]{2,1,0:T(8,128)(2,1)} %get-tuple-element.35) | copy-start | bytes 1327108
  248.6 1.7 copy-start.25
  248.6 2.5 copy-start.26
  252.7 1.6 copy-start.29
  254.3 1.5 copy-start.33

commit v3 on v2

--- a/solution.py
+++ b/solution.py
@@ -127,10 +127,10 @@
             remote(
                 src.at[block + 1 - core], held.at[d], send_a.at[d], recv_a.at[d], {"fsdp": partner}
             ).start()
-    for src, dst, extra in groups["fold"]:
-        up_buf, up_sum, down_buf, down_sum, up_send, up_recv, down_send, down_recv = extra
-        for k in range(seq_n - 1):
-            t = seq_n - 1 - k
+    for k in range(seq_n - 1):
+        t = seq_n - 1 - k
+        for src, dst, extra in groups["fold"]:
+            up_buf, up_sum, down_buf, down_sum, up_send, up_recv, down_send, down_recv = extra
 
             @pl.when(z == 0)
             def _():
@@ -199,11 +199,9 @@
     for d in range(1, seq_n):
         for src, dst, extra in groups["gather"]:
             line_step(dst, extra, d)
-        for src, dst, extra in groups["spread"]:
-            send_a, recv_a, send_b, recv_b, own = extra
-            for e in range(1, pairs):
-                if e % (seq_n - 1) != d % (seq_n - 1):
-                    continue
+        for e in range(1, pairs) if d == max(seq_n - 2, 1) else ():
+            for src, dst, extra in groups["spread"]:
+                send_a, recv_a, send_b, recv_b, own = extra
                 origin = ((chip + pairs - e) % pairs) * 2 + core
                 remote(src, dst.at[origin], send_a.at[e], recv_a.at[e], {"fsdp": partner}).wait_recv()
                 copy = remote(
@@ -228,7 +226,13 @@
                 down_sum[k] = (src[k].astype(f32) + down_buf[k].astype(f32)).astype(src.dtype)
                 remote(down_sum.at[k], down_buf.at[k], down_send.at[k], down_recv.at[k], down).start()
 
-    for src, dst, extra in groups["grad"]:
+    for j in range(len(groups["grad"]) + seq_n - 1):
+        for d in range(1, seq_n):
+            if 0 <= j - d < len(groups["grad"]):
+                line_step(groups["grad"][j - d][1], groups["grad"][j - d][2][6:10], d)
+        if j >= len(groups["grad"]):
+            continue
+        src, dst, extra = groups["grad"][j]
         held, total, send_a, recv_a, send_b, recv_b = extra[:6]
         value = total[0].astype(f32)
         for d in range(1, pairs):
@@ -238,9 +242,6 @@
             value = value + extra[10][d].astype(f32)
         dst[z] = value.astype(src.dtype)
         line_start(dst, extra[6:10], dst.at[z])
-    for d in range(1, seq_n):
-        for src, dst, extra in groups["grad"]:
-            line_step(dst, extra[6:10], d)
     for src, dst, extra in groups["fold"]:
         up_buf, up_sum, down_buf, down_sum, up_send, up_recv, down_send, down_recv = extra
         dst[...] = src[z].astype(f32)
@@ -395,12 +396,19 @@
     ff_part = ff // groups
     scale = HEAD_DIM ** (-0.5)
 
-    qkv_part = lax.dynamic_index_in_dim(
-        qkv_weight.reshape(shard, 3, groups, group_width), z, 2, keepdims=False
-    ).reshape(shard, 3 * group_width)
-    in_part = lax.dynamic_index_in_dim(
-        in_weight.reshape(shard, 2, groups, ff_part), z, 2, keepdims=False
-    ).reshape(shard, 2 * ff_part)
+    def pick(weight, sections, section):
+        part = None
+        for g in range(groups):
+            columns = [
+                weight[:, (j * groups + g) * section : (j * groups + g + 1) * section]
+                for j in range(sections)
+            ]
+            own = jnp.concatenate(columns, axis=1)
+            part = own if part is None else jnp.where(z == g, own, part)
+        return part
+
+    qkv_part = pick(qkv_weight, 3, group_width)
+    in_part = pick(in_weight, 2, ff_part)
     down_part = lax.dynamic_slice_in_dim(down_weight, z * ff_part, ff_part, 0).T
     gains = jnp.stack([norm1_gain, norm2_gain])
     own_tokens = tokens.reshape(rows, width)
@@ -452,12 +460,14 @@
     )
 
     def to_rows(heads):
-        return heads.transpose(0, 2, 1, 3).reshape(seq_dev * length, group_width)
+        return jnp.concatenate([heads[:, h] for h in range(local_heads)], axis=-1).reshape(
+            seq_dev * length, group_width
+        )
 
     (mixed,) = exchange(["swap"], [spans(to_rows(attended))], 1)
-    mixed = jnp.swapaxes(mixed, 0, 1).reshape(rows, width)
+    w_out = w_out.reshape(groups, group_width, width)
     inputs = own_tokens.astype(f32)
-    residual = inputs + dot(mixed, w_out)
+    residual = inputs + jnp.einsum("grd,gdw->rw", mixed, w_out, preferred_element_type=f32)
     normed_two, scaled_two, inverse_two = layer_norm(residual, gain_two)
     normed_two = normed_two.astype(low)
     (normed_full,) = exchange(["gather"], [normed_two], 2)
@@ -473,20 +483,14 @@
     ).astype(low)
     ffn_part = dot(gated, w_down, 1, 1).astype(low)
     normed_grad_part = dot(lifted_grad, w_in, 1, 1).astype(low)
-    ffn_parts, normed_grad_parts = exchange(
-        ["fold", "fold"], [spans(ffn_part), spans(normed_grad_part)], 3
-    )
-    block_out = (residual + ffn_parts).astype(low)
-    normed_two_grad = normed_grad_parts
+    (normed_two_grad,) = exchange(["fold"], [spans(normed_grad_part)], 3)
     gain_two_grad = jnp.sum(normed_two_grad * scaled_two, axis=0)
     residual_grad = own_cotangent.astype(f32) + norm_back(
         normed_two_grad, scaled_two, inverse_two, gain_two
     )
     residual_low = residual_grad.astype(low)
-    mixed_grad = dot(residual_low, w_out, 1, 1).astype(low)
-    (head_grad,) = exchange(
-        ["swap"], [jnp.swapaxes(mixed_grad.reshape(rows, groups, group_width), 0, 1)], 4
-    )
+    mixed_grad = jnp.einsum("rw,gdw->grd", residual_low, w_out, preferred_element_type=f32)
+    (head_grad,) = exchange(["swap"], [mixed_grad.astype(low)], 4)
     head_grad = whole(head_grad).reshape(seq_dev, length, local_heads, HEAD_DIM)
     head_grad = head_grad.transpose(0, 2, 1, 3)
     delta = jnp.sum(head_grad.astype(f32) * attended.astype(f32), axis=-1, keepdims=True)
@@ -509,13 +513,14 @@
     qkv_term = dot(normed_one, qkv_grad, 0, 0).astype(low)
     in_term = dot(normed_full, lifted_grad, 0, 0).astype(low)
     down_term = dot(all_cot, gated, 0, 0).astype(low)
-    out_term = dot(mixed, residual_low, 0, 0).astype(low)
+    out_term = jnp.einsum("grd,rw->gdw", mixed, residual_low, preferred_element_type=f32)
+    out_term = out_term.astype(low).reshape(width, width)
     gain_terms = jnp.stack(
         [gain_one_grad.reshape(fsdp_n, shard), gain_two_grad.reshape(fsdp_n, shard)], axis=1
     )
     parts = exchange(
-        ["fold", "grad", "grad", "grad", "grad", "grad"],
-        [spans(normed_one_grad_part.astype(low))]
+        ["fold", "fold", "grad", "grad", "grad", "grad", "grad"],
+        [spans(normed_one_grad_part.astype(low)), spans(ffn_part)]
         + [t.reshape(fsdp_n, shard, t.shape[1]) for t in (qkv_term, in_term, down_term, out_term)]
         + [gain_terms],
         5,
@@ -525,19 +530,21 @@
     input_grad = (
         residual_grad + norm_back(normed_one_grad, scaled_one, inverse_one, gain_one)
     ).astype(low)
-    qkv_all, in_all, down_all, out_all, gain_all = parts[1:]
-    qkv_out = (
-        qkv_all.reshape(groups, shard, 3, group_width)
-        .transpose(1, 2, 0, 3)
-        .reshape(shard, 3 * width)
-        .astype(f32)
-    )
-    in_out = (
-        in_all.reshape(groups, shard, 2, ff_part)
-        .transpose(1, 2, 0, 3)
-        .reshape(shard, 2 * ff)
-        .astype(f32)
-    )
+    block_out = (residual + parts[1]).astype(low)
+    qkv_all, in_all, down_all, out_all, gain_all = parts[2:]
+
+    def columns_of(stack, sections, section):
+        return jnp.concatenate(
+            [
+                stack[g][:, j * section : (j + 1) * section]
+                for j in range(sections)
+                for g in range(groups)
+            ],
+            axis=1,
+        ).astype(f32)
+
+    qkv_out = columns_of(qkv_all, 3, group_width)
+    in_out = columns_of(in_all, 2, ff_part)
     down_out = down_all.transpose(0, 2, 1).reshape(ff, shard).astype(f32)
     out_out = jnp.sum(out_all.astype(f32), axis=0)
     gain_out = jnp.sum(gain_all, axis=0)

time: 257 us -> 248 us (0.965)
  local copies, waits for them, and re-layouts: 35.4 us -> 26.8 us
  other arithmetic: 15.2 us -> 20.9 us
  Pallas kernels: 180 us -> 175 us
    slice x0 -> x14, local copies, waits for them, and re-layouts: none -> 7.78 us  [the longest x4 5.47 us: to_rows(): heads[:, h]]
    convert_element_type x7 -> x1, local copies, waits for them, and re-layouts: 7.73 us -> 1.77 us  [local(): head_grad, = exchange(['swap'], [mixed_grad.astype(low)], 4)]
    reshape x5 -> x0, local copies, waits for them, and re-layouts: 5.68 us -> none  [the longest x1 1.77 us: local(): mixed_grad.reshape(rows, groups, group_width)]
    pallas_call x6, Pallas kernels: 180 us -> 175 us  [exchange(): pl.pallas_call(functools.partial(exchange_kernel, tuple(kinds), seq_n, fs...]
    dot_general x0 -> x3, matrix products: none -> 4.51 us  [the longest x1 1.82 us: local(): jnp.einsum('grd,gdw->rw', mixed, w_out, preferred_element_type=f32)]
    dot_general x12 -> x9, matrix products: 17.4 us -> 13.7 us  [dot(): lax.dot_general(left, right, (((left_dim,), (right_dim,)), ((), ())), pre...]
    another operation x2 -> x0, local copies, waits for them, and re-layouts: 3.43 us -> none  [spans(): jnp.swapaxes(full.reshape(seq_dev, groups, span_len, w), 0, 1)]
where the time goes in v3:
time: 248 us; the launch traced here: 247 us
  Pallas kernels  175 us (71%)
  local copies, waits for them, and re-layouts  26.8 us (11%)
  matrix products  23.1 us (9%)
  other arithmetic  20.9 us (8%)
    pallas_call x6, Pallas kernels, exchange(): pl.pallas_call(functools.partial(exchange_kernel, tuple(kinds), seq_n, fs...  175 us
    dot_general x9, matrix products, dot(): lax.dot_general(left, right, (((left_dim,), (right_dim,)), ((), ())), pre...  13.7 us
    slice x4, local copies, waits for them, and re-layouts, to_rows(): heads[:, h]  5.47 us

profile of v3, /device:TPU:0, one launch (start us, length us, event | category | flops | bytes accessed | tf_op | source)
XLA Modules:
  0.0 247.2 jit_solution(831541890109633551)
XLA Ops:
  0.7 1.4 fusion.84
  2.1 0.8 maximum_select_fusion.refs_3_
  3.1 0.8 maximum_select_fusion.3.refs_5_
  4.0 0.7 dynamic-slice_bitcast_fusion.refs_6_
  4.7 0.5 pad_maximum_fusion.16.refs_7_
  5.2 36.4 %exchange_0.1 = (bf16[4,128,768]{2,1,0:T(8,128)(2,1)}, bf16[4,128,768]{2,1,0:T(8,128)(2,1)}, s32[4,1,128]{2,1,0:T(1,128)}, bf16[8,96,576]{2,1,0:T(8,128)(2,1)}, ...) custom-call(bf16[128,768]{1,0:T(8,128)(2,1)} %bitcast.179, ...), custom_call_target="tpu_custom_call" | custom-call | tf_op jit(solution)/shard_map/exchange_0/pallas_call | solution.py:312
  41.7 1.4 convert_reduce_fusion
  43.1 1.5 multiply_reduce_fusion.2
  44.8 0.6 copy.52
  45.4 0.8 fusion.12
  46.3 0.6 copy-done.47
  47.0 0.9 fusion.71
  48.1 0.6 multiply_reduce_fusion
  48.8 0.5 exponential_reduce_fusion
  49.3 0.6 fusion.6
  50.0 0.7 copy-done.13
  50.7 0.7 fusion.85
  51.3 1.6 copy.55
  52.9 1.6 copy.56
  54.5 1.6 copy.57
  56.1 1.9 pad_maximum_fusion.4.refs_0_
  58.0 9.2 %exchange_1.1 = bf16[4,128,192]{2,1,0:T(8,128)(2,1)} custom-call(bf16[4,128,192]{2,1,0:T(8,128)(2,1)} %pad_maximum_fusion.4.refs_0_), custom_call_target="tpu_custom_call" | custom-call | tf_op jit(solution)/shard_map/exchange_1/pallas_call | solution.py:312
  67.2 1.8 fusion.94
  69.0 0.7 copy-done.1
  69.9 0.5 add_rsqrt_fusion.1
  70.5 1.8 multiply_convert_fusion.5.refs_0_
  72.3 20.3 %exchange_2.1 = bf16[4,128,768]{2,1,0:T(8,128)(2,1)} custom-call(bf16[128,768]{1,0:T(8,128)(2,1)} %multiply_convert_fusion.5.refs_0_), custom_call_target="tpu_custom_call" | custom-call | tf_op jit(solution)/shard_map/exchange_2/pallas_call | solution.py:312
  92.7 2.2 fusion.96
  94.9 2.6 %multiply_convert_fusion.3 = (bf16[512,288]{0,1:T(8,128)(2,1)}, f32[512,288]{0,1:T(8,128)S(1)}, bf16[512,288]{0,1:T(8,128)(2,1)S(1)}, f32[512,288]{0,1:T(8,128)S(1)}) fusion(f32[512,576]{0,1:T(8,128)S(1)} %fusion.96, bf16[512,768]{1,0:T(8,128)(2,1)S(1)} %bitcast.200, bf16[768,288]{1,0:T(8,128)(2,1)S(1)} %bitcast.205), kind=kOutput, calls=%fused_computation.54 | convolution fusion | flops 237846528 | bytes 4177920 | tf_op jit(solution)/shard_map/dot_general | solution.py:368
  97.6 1.7 convolution_convert_fusion.3
  99.3 24.3 %exchange_3.1 = f32[128,768]{1,0:T(8,128)} custom-call(bf16[4,128,768]{2,1,0:T(8,128)(2,1)} %bitcast.202), custom_call_target="tpu_custom_call" | custom-call | tf_op jit(solution)/shard_map/exchange_3/pallas_call | solution.py:312
  123.7 1.4 multiply_reduce_fusion.3
  125.1 1.4 multiply_add_fusion
  126.5 0.7 copy-done.4
  127.3 1.1 convolution_convert_fusion.8
  128.4 1.8 copy.59
  130.2 7.9 %exchange_4.1 = bf16[4,128,192]{2,1,0:T(8,128)(2,1)} custom-call(bf16[4,128,192]{2,1,0:T(8,128)(2,1)} %bitcast.194), custom_call_target="tpu_custom_call" | custom-call | tf_op jit(solution)/shard_map/exchange_4/pallas_call | solution.py:312
  138.1 1.8 copy.60
  139.9 1.7 reshape_reshape_transpose_reshape.3
  141.6 1.1 multiply_reduce_fusion.4
  142.7 2.0 multiply_convert_fusion
  144.7 0.6 fusion.10
  146.0 0.4 copy-done.36
  146.9 0.7 fusion.5
  147.6 0.5 copy-done.8
  148.4 2.1 multiply_reduce_fusion.1
  150.7 0.6 pad_maximum_fusion.15.refs_6_
  151.3 1.5 convolution_convert_fusion
  152.9 0.6 convolution_convert_fusion.1
  153.5 1.3 copy.66
  154.9 1.8 convolution_convert_fusion.2
  156.6 1.3 copy.65
  158.0 0.4 convolution_convert_fusion.5
  158.4 1.1 copy.67
  159.5 1.5 convolution_convert_fusion.4
  160.9 76.8 %exchange_5.1 = (f32[128,768]{1,0:T(8,128)}, f32[128,768]{1,0:T(8,128)}, bf16[4,96,576]{2,1,0:T(8,128)(2,1)}, bf16[4,96,576]{2,1,0:T(8,128)(2,1)}, bf16[4,96,288...) custom-call(bf16[4,128,768]{2,1,0:T(8,128)(2,1)} %bitcast.204, bf16[4,128,768]{2,1,0:T(8,128)(2,1)} %bitcast.188, ...), custom_call_target="tpu_custom_call" | custom-call | tf_op jit(solution)/shard_map/exchange_5/pallas_call | solution.py:312
  237.8 1.1 slice_bitcast_fusion.2
  239.6 1.0 convert_element_type.278
  241.2 1.0 convert_element_type.276
  242.6 1.1 reshape.578
  244.2 0.9 fusion.47
  245.1 0.8 convert_reduce_fusion.1
  245.9 0.7 fusion.45
  246.6 0.5 slice_bitcast_fusion.13
  (146 shorter events, 5.0 us)
Async XLA Ops:
  0.6 3.3 %copy-start = (bf16[1152,96]{0,1:T(8,128)(2,1)S(1)}, bf16[1152,96]{0,1:T(8,128)(2,1)}, u32[]{:S(2)}) copy-start(bf16[1152,96]{0,1:T(8,128)(2,1)} %param.16) | copy-start | bytes 663556
  0.6 2.3 copy-start.27
  2.0 2.7 %copy-start.48 = (bf16[96]{0:T(256)(128)(2,1)S(1)}, bf16[96]{0:T(256)(128)(2,1)}, u32[]{:S(2)}) copy-start(bf16[96]{0:T(256)(128)(2,1)} %param.14) | copy-start | bytes 580
  2.1 2.6 %copy-start.49 = (bf16[96]{0:T(256)(128)(2,1)S(1)}, bf16[96]{0:T(256)(128)(2,1)}, u32[]{:S(2)}) copy-start(bf16[96]{0:T(256)(128)(2,1)} %param.11) | copy-start | bytes 580
  41.6 3.0 %copy-start.41 = (bf16[8,2,96]{2,1,0:T(2,128)(2,1)S(1)}, bf16[8,2,96]{2,1,0:T(2,128)(2,1)}, u32[]{:S(2)}) copy-start(bf16[8,2,96]{2,1,0:T(2,128)(2,1)} %get-tuple-element.24) | copy-start | bytes 9220
  41.7 3.1 %copy-start.16 = (bf16[8,96,576]{2,1,0:T(8,128)(2,1)S(1)}, bf16[8,96,576]{2,1,0:T(8,128)(2,1)}, u32[]{:S(2)}) copy-start(bf16[8,96,576]{2,1,0:T(8,128)(2,1)} %get-tuple-element.25) | copy-start | bytes 2654212
  41.7 3.7 %copy-start.7 = (bf16[4,128,768]{2,1,0:T(8,128)(2,1)S(1)}, bf16[4,128,768]{2,1,0:T(8,128)(2,1)}, u32[]{:S(2)}) copy-start(bf16[4,128,768]{2,1,0:T(8,128)(2,1)} %get-tuple-element.23) | copy-start | bytes 2359300
  43.1 3.1 %copy-start.43 = (f32[512]{0:T(512)}, f32[512]{0:T(512)S(1)}, u32[]{:S(2)}) copy-start(f32[512]{0:T(512)S(1)} %get-tuple-element.126) | copy-start | bytes 6148
  44.6 1.6 copy-start.45
  46.2 3.1 %copy-start.12 = (f32[512,3,3,64]{0,3,2,1:T(8,128)}, f32[512,3,3,64]{0,3,2,1:T(8,128)S(1)}, u32[]{:S(2)}) copy-start(f32[512,3,3,64]{0,3,2,1:T(8,128)S(1)} %fusion.12) | copy-start | bytes 3538948
  46.3 0.7 copy-start.47
  48.0 0.7 copy-start.19
  48.0 0.7 copy-start.21
  48.1 0.7 copy-start.23
  50.0 0.7 copy-start.13
  69.0 0.8 copy-start.1
  92.6 2.2 copy-start.25
  92.6 2.2 copy-start.28
  94.9 2.7 %copy-start.18 = (bf16[8,96,576]{2,1,0:T(8,128)(2,1)S(1)}, bf16[8,96,576]{2,1,0:T(8,128)(2,1)}, u32[]{:S(2)}) copy-start(bf16[8,96,576]{2,1,0:T(8,128)(2,1)} %get-tuple-element.30) | copy-start | bytes 2654212
  97.5 1.9 copy-start.50
  97.6 1.7 copy-start.34
  123.7 3.6 %copy-start.6 = (bf16[8,96,768]{2,1,0:T(8,128)(2,1)S(1)}, bf16[8,96,768]{2,1,0:T(8,128)(2,1)}, u32[]{:S(2)}) copy-start(bf16[8,96,768]{2,1,0:T(8,128)(2,1)} %get-tuple-element.27) | copy-start | bytes 3538948
  126.5 0.7 copy-start.4
  142.6 2.0 copy-start.22
  142.7 2.0 copy-start.24
  144.7 0.9 copy-start.20
  145.6 0.8 copy-start.36
  145.9 0.9 copy-start.10
  146.6 1.1 copy-start.37
  146.9 0.7 copy-start.39
  146.9 1.2 copy-start.8
  146.9 1.5 copy-start.17
  146.9 1.5 copy-start.44
  146.9 1.5 copy-start.46
  148.4 2.9 %copy-start.5 = (f32[128,768]{1,0:T(8,128)S(1)}, f32[128,768]{1,0:T(8,128)}, u32[]{:S(2)}) copy-start(f32[128,768]{1,0:T(8,128)} %copy-done.4) | copy-start | bytes 1179652
  148.4 2.9 %copy-start.11 = (bf16[4,128,192]{2,1,0:T(8,128)(2,1)S(1)}, bf16[4,128,192]{2,1,0:T(8,128)(2,1)}, u32[]{:S(2)}) copy-start(bf16[4,128,192]{2,1,0:T(8,128)(2,1)} %exchange_1.1) | copy-start | bytes 589828
  150.5 2.3 copy-start.9
  150.5 2.3 copy-start.35
  150.5 2.3 copy-start.51
  153.5 1.3 copy-start.38
  153.5 1.3 copy-start.40
  156.6 1.4 copy-start.15
  156.6 1.4 copy-start.26
  158.0 1.5 copy-start.29
  239.0 1.6 copy-start.31
  240.7 1.5 copy-start.33
  242.1 1.5 copy-start.3
  242.1 1.8 copy-start.14
  242.6 2.5 %copy-start.30 = (bf16[4,96,768]{2,1,0:T(8,128)(2,1)S(1)}, bf16[4,96,768]{2,1,0:T(8,128)(2,1)}, u32[]{:S(2)}) copy-start(bf16[4,96,768]{2,1,0:T(8,128)(2,1)} %get-tuple-element.34) | copy-start | bytes 1769476
  243.6 2.3 copy-start.2
  243.6 2.3 copy-start.32
  244.2 2.4 copy-start.42

commit v4 on v3

--- a/solution.py
+++ b/solution.py
@@ -15,7 +15,7 @@
 theta = 160000.0
 
 
-EXTRA = {"gather": 4, "swap": 3, "spread": 5, "fold": 8, "grad": 11}
+EXTRA = {"gather": 4, "swap": 3, "spread": 5, "fold": 8, "grad": 11, "reduce": 11}
 
 
 def exchange_kernel(kinds, seq_n, fsdp_n, *refs):
@@ -30,8 +30,8 @@
     chip = f // 2
     core = f % 2
     partner = chip * 2 + 1 - core
-    on_seq = any(kind != "spread" for kind in kinds)
-    on_fsdp = any(kind in ("spread", "grad") for kind in kinds)
+    on_seq = any(kind not in ("spread", "reduce") for kind in kinds)
+    on_fsdp = any(kind in ("spread", "grad", "reduce") for kind in kinds)
 
     barrier = pltpu.get_barrier_semaphore()
     waits = 0
@@ -120,13 +120,39 @@
                 block = src if d == 0 else dst.at[lax.rem(z + d, seq_n)]
                 remote(block, dst.at[z], down_send.at[d], down_recv.at[d + 1], down).wait_send()
 
-    for src, dst, extra in groups["grad"]:
+    lower = z * 2 < seq_n
+
+    def fold_steps(k, first):
+        t = seq_n - 1 - k
+        for src, dst, extra in groups["fold"]:
+            up_buf, up_sum, down_buf, down_sum, up_send, up_recv, down_send, down_recv = extra
+            near_up = lower if first else jnp.logical_not(lower)
+
+            @pl.when(jnp.logical_and(near_up, jnp.logical_and(z > 0, z < t)))
+            def _():
+                remote(src.at[t], up_buf.at[t], up_send.at[t], up_recv.at[t], up).wait_recv()
+                up_sum[t] = (src[t].astype(f32) + up_buf[t].astype(f32)).astype(src.dtype)
+                remote(up_sum.at[t], up_buf.at[t], up_send.at[t], up_recv.at[t], up).start()
+
+            @pl.when(
+                jnp.logical_and(
+                    jnp.logical_not(near_up), jnp.logical_and(z < seq_n - 1, z > k)
+                )
+            )
+            def _():
+                remote(src.at[k], down_buf.at[k], down_send.at[k], down_recv.at[k], down).wait_recv()
+                down_sum[k] = (src[k].astype(f32) + down_buf[k].astype(f32)).astype(src.dtype)
+                remote(down_sum.at[k], down_buf.at[k], down_send.at[k], down_recv.at[k], down).start()
+
+    for src, dst, extra in groups["grad"] + groups["reduce"]:
         held, total, send_a, recv_a, send_b, recv_b = extra[:6]
         for d in range(pairs):
             block = ((chip + d) % pairs) * 2
             remote(
                 src.at[block + 1 - core], held.at[d], send_a.at[d], recv_a.at[d], {"fsdp": partner}
             ).start()
+    for src, dst, extra in groups["gather"]:
+        line_start(dst, extra, src)
     for k in range(seq_n - 1):
         t = seq_n - 1 - k
         for src, dst, extra in groups["fold"]:
@@ -140,8 +166,6 @@
             def _():
                 remote(src.at[k], down_buf.at[k], down_send.at[k], down_recv.at[k], down).start()
 
-    for src, dst, extra in groups["gather"]:
-        line_start(dst, extra, src)
     for src, dst, extra in groups["swap"]:
         send, recv, own = extra
         for d in range(1, seq_n):
@@ -176,7 +200,7 @@
         finish.append(local_copy.wait)
     for src, dst, extra in groups["gather"]:
         dst[z] = src[...]
-    for src, dst, extra in groups["grad"]:
+    for src, dst, extra in groups["grad"] + groups["reduce"]:
         held, total, send_a, recv_a, send_b, recv_b = extra[:6]
         for d in list(range(1, pairs)) + [0]:
             block = ((chip + d) % pairs) * 2
@@ -209,22 +233,9 @@
                 )
                 copy.start()
                 finish.append(copy.wait_send)
-        k = d - 1
-        t = seq_n - 1 - k
-        for src, dst, extra in groups["fold"]:
-            up_buf, up_sum, down_buf, down_sum, up_send, up_recv, down_send, down_recv = extra
-
-            @pl.when(jnp.logical_and(z > 0, z < t))
-            def _():
-                remote(src.at[t], up_buf.at[t], up_send.at[t], up_recv.at[t], up).wait_recv()
-                up_sum[t] = (src[t].astype(f32) + up_buf[t].astype(f32)).astype(src.dtype)
-                remote(up_sum.at[t], up_buf.at[t], up_send.at[t], up_recv.at[t], up).start()
-
-            @pl.when(jnp.logical_and(z < seq_n - 1, z > k))
-            def _():
-                remote(src.at[k], down_buf.at[k], down_send.at[k], down_recv.at[k], down).wait_recv()
-                down_sum[k] = (src[k].astype(f32) + down_buf[k].astype(f32)).astype(src.dtype)
-                remote(down_sum.at[k], down_buf.at[k], down_send.at[k], down_recv.at[k], down).start()
+        fold_steps(d - 1, True)
+    for k in range(seq_n - 1):
+        fold_steps(k, False)
 
     for j in range(len(groups["grad"]) + seq_n - 1):
         for d in range(1, seq_n):
@@ -242,6 +253,15 @@
             value = value + extra[10][d].astype(f32)
         dst[z] = value.astype(src.dtype)
         line_start(dst, extra[6:10], dst.at[z])
+    for src, dst, extra in groups["reduce"]:
+        total, send_b, recv_b = extra[1], extra[4], extra[5]
+        value = total[0].astype(f32)
+        for d in range(1, pairs):
+            remote(
+                total.at[d], extra[10].at[d], send_b.at[d], recv_b.at[d], {"fsdp": partner}
+            ).wait_recv()
+            value = value + extra[10][d].astype(f32)
+        dst[...] = value.astype(src.dtype)
     for src, dst, extra in groups["fold"]:
         up_buf, up_sum, down_buf, down_sum, up_send, up_recv, down_send, down_recv = extra
         dst[...] = src[z].astype(f32)
@@ -304,7 +324,9 @@
             shape = (fsdp_n,) + array.shape
             scratch += [dma((pairs,))] * 4 + [dma((1,))]
         else:
-            shape = (seq_n,) + array.shape[1:]
+            shape = array.shape[1:]
+            if kind == "grad":
+                shape = (seq_n,) + shape
             half = pltpu.VMEM((pairs,) + array.shape[1:], dtype)
             scratch += [half] * 2 + [dma((pairs,))] * 4 + [dma((seq_n,))] * 4 + [half]
         results.append(jax.ShapeDtypeStruct(shape, dtype))
@@ -483,14 +505,28 @@
     ).astype(low)
     ffn_part = dot(gated, w_down, 1, 1).astype(low)
     normed_grad_part = dot(lifted_grad, w_in, 1, 1).astype(low)
-    (normed_two_grad,) = exchange(["fold"], [spans(normed_grad_part)], 3)
+    in_term = dot(normed_full, lifted_grad, 0, 0).astype(low)
+    down_term = dot(all_cot, gated, 0, 0).astype(low)
+
+    def by_owner(term):
+        return term.reshape(fsdp_n, shard, term.shape[1])
+
+    normed_two_grad, in_owned, down_owned = exchange(
+        ["fold", "reduce", "reduce"],
+        [spans(normed_grad_part), by_owner(in_term), by_owner(down_term)],
+        3,
+    )
     gain_two_grad = jnp.sum(normed_two_grad * scaled_two, axis=0)
     residual_grad = own_cotangent.astype(f32) + norm_back(
         normed_two_grad, scaled_two, inverse_two, gain_two
     )
     residual_low = residual_grad.astype(low)
     mixed_grad = jnp.einsum("rw,gdw->grd", residual_low, w_out, preferred_element_type=f32)
-    (head_grad,) = exchange(["swap"], [mixed_grad.astype(low)], 4)
+    out_term = jnp.einsum("grd,rw->gdw", mixed, residual_low, preferred_element_type=f32)
+    out_term = out_term.astype(low).reshape(width, width)
+    head_grad, out_owned = exchange(
+        ["swap", "reduce"], [mixed_grad.astype(low), by_owner(out_term)], 4
+    )
     head_grad = whole(head_grad).reshape(seq_dev, length, local_heads, HEAD_DIM)
     head_grad = head_grad.transpose(0, 2, 1, 3)
     delta = jnp.sum(head_grad.astype(f32) * attended.astype(f32), axis=-1, keepdims=True)
@@ -511,18 +547,13 @@
     gain_one_grad = jnp.sum(normed_one_grad_part * scaled_full, axis=0)
 
     qkv_term = dot(normed_one, qkv_grad, 0, 0).astype(low)
-    in_term = dot(normed_full, lifted_grad, 0, 0).astype(low)
-    down_term = dot(all_cot, gated, 0, 0).astype(low)
-    out_term = jnp.einsum("grd,rw->gdw", mixed, residual_low, preferred_element_type=f32)
-    out_term = out_term.astype(low).reshape(width, width)
     gain_terms = jnp.stack(
         [gain_one_grad.reshape(fsdp_n, shard), gain_two_grad.reshape(fsdp_n, shard)], axis=1
     )
     parts = exchange(
-        ["fold", "fold", "grad", "grad", "grad", "grad", "grad"],
+        ["fold", "fold", "gather", "gather", "gather", "grad", "grad"],
         [spans(normed_one_grad_part.astype(low)), spans(ffn_part)]
-        + [t.reshape(fsdp_n, shard, t.shape[1]) for t in (qkv_term, in_term, down_term, out_term)]
-        + [gain_terms],
+        + [in_owned, down_owned, out_owned, by_owner(qkv_term), gain_terms],
         5,
     )
     normed_one_grad = parts[0]
@@ -531,7 +562,7 @@
         residual_grad + norm_back(normed_one_grad, scaled_one, inverse_one, gain_one)
     ).astype(low)
     block_out = (residual + parts[1]).astype(low)
-    qkv_all, in_all, down_all, out_all, gain_all = parts[2:]
+    in_all, down_all, out_all, qkv_all, gain_all = parts[2:]
 
     def columns_of(stack, sections, section):
         return jnp.concatenate(

time: 248 us -> 236 us (0.952)
  Pallas kernels: 175 us -> 155 us
  matrix products: 23.1 us -> 27.3 us
  local copies, waits for them, and re-layouts: 26.8 us -> 29.4 us
    pallas_call x6, Pallas kernels: 175 us -> 155 us  [exchange(): pl.pallas_call(functools.partial(exchange_kernel, tuple(kinds), seq_n, fs...]
    dot_general x9, matrix products: 13.7 us -> 17.9 us  [dot(): lax.dot_general(left, right, (((left_dim,), (right_dim,)), ((), ())), pre...]
    unnamed x104 -> x90, local copies, waits for them, and re-layouts: 4.75 us -> 5.37 us
where the time goes in v4:
time: 236 us; the launch traced here: 235 us
  Pallas kernels  155 us (66%)
  local copies, waits for them, and re-layouts  29.4 us (12%)
  matrix products  27.3 us (12%)
  other arithmetic  22.2 us (9%)
    pallas_call x6, Pallas kernels, exchange(): pl.pallas_call(functools.partial(exchange_kernel, tuple(kinds), seq_n, fs...  155 us
    dot_general x9, matrix products, dot(): lax.dot_general(left, right, (((left_dim,), (right_dim,)), ((), ())), pre...  17.9 us
    slice x4, local copies, waits for them, and re-layouts, to_rows(): heads[:, h]  5.47 us
    unnamed x90, local copies, waits for them, and re-layouts  5.37 us

profile of v4, /device:TPU:0, one launch (start us, length us, event | category | flops | bytes accessed | tf_op | source)
XLA Modules:
  0.0 235.2 jit_solution(10385993504822533095)
XLA Ops:
  0.7 1.4 fusion.84
  2.1 0.8 maximum_select_fusion.refs_3_
  3.1 0.8 maximum_select_fusion.3.refs_5_
  4.0 0.7 dynamic-slice_bitcast_fusion.refs_6_
  4.7 0.5 pad_maximum_fusion.16.refs_7_
  5.2 36.4 %exchange_0.1 = (bf16[4,128,768]{2,1,0:T(8,128)(2,1)}, bf16[4,128,768]{2,1,0:T(8,128)(2,1)}, s32[4,1,128]{2,1,0:T(1,128)}, bf16[8,96,576]{2,1,0:T(8,128)(2,1)}, ...) custom-call(bf16[128,768]{1,0:T(8,128)(2,1)} %bitcast.179, ...), custom_call_target="tpu_custom_call" | custom-call | tf_op jit(solution)/shard_map/exchange_0/pallas_call | solution.py:334
  41.6 1.4 convert_reduce_fusion
  43.1 1.5 multiply_reduce_fusion.2
  44.7 0.6 copy.52
  45.4 0.8 fusion.12
  46.3 0.6 copy-done.42
  46.9 0.9 fusion.71
  48.0 0.6 multiply_reduce_fusion
  48.7 0.5 exponential_reduce_fusion
  49.3 0.6 fusion.6
  49.9 0.7 copy-done.12
  50.6 0.7 fusion.85
  51.2 1.6 copy.55
  52.8 1.6 copy.56
  54.4 1.6 copy.57
  56.0 1.9 pad_maximum_fusion.4.refs_0_
  57.9 9.2 %exchange_1.1 = bf16[4,128,192]{2,1,0:T(8,128)(2,1)} custom-call(bf16[4,128,192]{2,1,0:T(8,128)(2,1)} %pad_maximum_fusion.4.refs_0_), custom_call_target="tpu_custom_call" | custom-call | tf_op jit(solution)/shard_map/exchange_1/pallas_call | solution.py:334
  67.1 1.8 fusion.94
  68.9 0.7 copy-done.1
  69.8 0.5 add_rsqrt_fusion.1
  70.5 1.8 multiply_convert_fusion.5.refs_0_
  72.3 20.4 %exchange_2.1 = bf16[4,128,768]{2,1,0:T(8,128)(2,1)} custom-call(bf16[128,768]{1,0:T(8,128)(2,1)} %multiply_convert_fusion.5.refs_0_), custom_call_target="tpu_custom_call" | custom-call | tf_op jit(solution)/shard_map/exchange_2/pallas_call | solution.py:334
  92.7 2.2 fusion.96
  94.9 2.9 %multiply_convert_fusion.3 = (bf16[512,288]{0,1:T(8,128)(2,1)S(1)}, f32[512,288]{0,1:T(8,128)}, bf16[512,288]{0,1:T(8,128)(2,1)}, f32[512,288]{0,1:T(8,128)}) fusion(f32[512,576]{0,1:T(8,128)S(1)} %fusion.96, bf16[512,768]{1,0:T(8,128)(2,1)S(1)} %bitcast.200, bf16[768,288]{1,0:T(8,128)(2,1)S(1)} %bitcast.205), kind=kOutput, calls=%fused_computation.54 | convolution fusion | flops 237846528 | bytes 4177920 | tf_op jit(solution)/shard_map/dot_general | solution.py:390
  97.8 0.7 copy-done.14
  98.5 1.2 convolution_convert_fusion.5
  99.7 2.1 copy.60
  101.8 1.3 multiply_convert_fusion.4
  103.1 0.7 copy-done.32
  103.8 2.8 %convolution_convert_fusion.2 = bf16[768,576]{0,1:T(8,128)(2,1)} fusion(bf16[512,768]{1,0:T(8,128)(2,1)} %bitcast.188, bf16[512,288]{0,1:T(8,128)(2,1)S(1)} %multiply_convert_fusion.4, bf16[512,288]{0,1:T(8,128)(2,1)} %get-tuple-element.59), kind=kOutput, calls=%fused_computation.13 | convolution fusion | flops 454606848 | bytes 2260992 | tf_op jit(solution)/shard_map/dot_general | solution.py:390
  106.6 2.3 copy.59
  108.8 3.1 %convolution_convert_fusion.3 = bf16[512,768]{1,0:T(8,128)(2,1)} fusion(bf16[768,576]{1,0:T(8,128)(2,1)} %bitcast.198, bf16[512,288]{0,1:T(8,128)(2,1)} %copy-done.32, bf16[512,288]{0,1:T(8,128)(2,1)} %get-tuple-element.59), kind=kOutput, calls=%fused_computation.14 | convolution fusion | flops 454557696 | bytes 2260992 | tf_op jit(solution)/shard_map/dot_general | solution.py:390
  111.9 21.3 %exchange_3.1 = (f32[128,768]{1,0:T(8,128)}, bf16[96,576]{1,0:T(8,128)(2,1)}, bf16[96,288]{1,0:T(8,128)(2,1)}) custom-call(bf16[4,128,768]{2,1,0:T(8,128)(2,1)} %bitcast.203, bf16[8,96,576]{2,1,0:T(8,128)(2,1)} %bitcast.183, bf16[8,96,288]{2,1,0:T(8,128)(2,1)} %bitcast.189), custom_call_target="tpu_custom_call" | custom-call | tf_op jit(solution)/shard_map/exchange_3/pallas_call | solution.py:334
  133.3 1.4 multiply_reduce_fusion.3
  134.7 1.5 multiply_add_fusion
  136.2 1.5 convolution_convert_fusion
  137.7 1.1 convolution_convert_fusion.8
  138.8 1.8 copy.61
  140.6 12.8 %exchange_4.1 = (bf16[4,128,192]{2,1,0:T(8,128)(2,1)}, bf16[96,768]{1,0:T(8,128)(2,1)}) custom-call(bf16[4,128,192]{2,1,0:T(8,128)(2,1)} %bitcast.194, bf16[8,96,768]{2,1,0:T(8,128)(2,1)} %bitcast.182), custom_call_target="tpu_custom_call" | custom-call | tf_op jit(solution)/shard_map/exchange_4/pallas_call | solution.py:334
  153.4 1.8 copy.63
  155.2 1.7 reshape_reshape_transpose_reshape.3
  156.9 1.1 multiply_reduce_fusion.4
  158.0 2.0 multiply_convert_fusion
  160.0 0.6 fusion.10
  162.3 0.7 fusion.5
  163.8 1.9 multiply_reduce_fusion.1
  165.8 0.6 pad_maximum_fusion.15.refs_6_
  166.4 1.6 convolution_convert_fusion.1
  168.1 1.3 copy.68
  169.4 1.5 convolution_convert_fusion.4
  170.9 54.9 %exchange_5.1 = (f32[128,768]{1,0:T(8,128)}, f32[128,768]{1,0:T(8,128)}, bf16[4,96,576]{2,1,0:T(8,128)(2,1)}, bf16[4,96,288]{2,1,0:T(8,128)(2,1)}, bf16[4,96,768...) custom-call(bf16[4,128,768]{2,1,0:T(8,128)(2,1)} %bitcast.202, bf16[4,128,768]{2,1,0:T(8,128)(2,1)} %bitcast.186, ...), custom_call_target="tpu_custom_call" | custom-call | tf_op jit(solution)/shard_map/exchange_5/pallas_call | solution.py:334
  225.8 1.1 slice_bitcast_fusion.2
  227.6 1.0 convert_element_type.278
  229.2 1.0 convert_element_type.276
  230.6 1.1 reshape.578
  232.3 0.9 fusion.47
  233.2 0.8 convert_reduce_fusion.1
  234.0 0.7 fusion.45
  234.7 0.5 slice_bitcast_fusion.13
  (132 shorter events, 5.7 us)
Async XLA Ops:
  0.6 3.3 %copy-start = (bf16[1152,96]{0,1:T(8,128)(2,1)S(1)}, bf16[1152,96]{0,1:T(8,128)(2,1)}, u32[]{:S(2)}) copy-start(bf16[1152,96]{0,1:T(8,128)(2,1)} %param.16) | copy-start | bytes 663556
  0.6 2.3 copy-start.25
  2.0 2.7 %copy-start.43 = (bf16[96]{0:T(256)(128)(2,1)S(1)}, bf16[96]{0:T(256)(128)(2,1)}, u32[]{:S(2)}) copy-start(bf16[96]{0:T(256)(128)(2,1)} %param.14) | copy-start | bytes 580
  2.1 2.6 %copy-start.44 = (bf16[96]{0:T(256)(128)(2,1)S(1)}, bf16[96]{0:T(256)(128)(2,1)}, u32[]{:S(2)}) copy-start(bf16[96]{0:T(256)(128)(2,1)} %param.11) | copy-start | bytes 580
  41.6 3.0 %copy-start.36 = (bf16[8,2,96]{2,1,0:T(2,128)(2,1)S(1)}, bf16[8,2,96]{2,1,0:T(2,128)(2,1)}, u32[]{:S(2)}) copy-start(bf16[8,2,96]{2,1,0:T(2,128)(2,1)} %get-tuple-element.29) | copy-start | bytes 9220
  41.6 3.1 %copy-start.16 = (bf16[8,96,576]{2,1,0:T(8,128)(2,1)S(1)}, bf16[8,96,576]{2,1,0:T(8,128)(2,1)}, u32[]{:S(2)}) copy-start(bf16[8,96,576]{2,1,0:T(8,128)(2,1)} %get-tuple-element.30) | copy-start | bytes 2654212
  41.6 3.7 %copy-start.7 = (bf16[4,128,768]{2,1,0:T(8,128)(2,1)S(1)}, bf16[4,128,768]{2,1,0:T(8,128)(2,1)}, u32[]{:S(2)}) copy-start(bf16[4,128,768]{2,1,0:T(8,128)(2,1)} %get-tuple-element.28) | copy-start | bytes 2359300
  43.1 3.1 %copy-start.38 = (f32[512]{0:T(512)}, f32[512]{0:T(512)S(1)}, u32[]{:S(2)}) copy-start(f32[512]{0:T(512)S(1)} %get-tuple-element.136) | copy-start | bytes 6148
  44.6 1.6 copy-start.40
  46.2 3.0 %copy-start.11 = (f32[512,3,3,64]{0,3,2,1:T(8,128)}, f32[512,3,3,64]{0,3,2,1:T(8,128)S(1)}, u32[]{:S(2)}) copy-start(f32[512,3,3,64]{0,3,2,1:T(8,128)S(1)} %fusion.12) | copy-start | bytes 3538948
  46.2 0.7 copy-start.42
  48.0 0.7 copy-start.18
  48.0 0.7 copy-start.20
  48.0 0.7 copy-start.22
  49.9 0.7 copy-start.12
  68.9 0.8 copy-start.1
  92.6 2.2 copy-start.24
  92.7 2.2 copy-start.26
  97.8 0.7 copy-start.14
  103.1 0.7 copy-start.32
  133.2 2.9 %copy-start.10 = (bf16[4,128,192]{2,1,0:T(8,128)(2,1)S(1)}, bf16[4,128,192]{2,1,0:T(8,128)(2,1)}, u32[]{:S(2)}) copy-start(bf16[4,128,192]{2,1,0:T(8,128)(2,1)} %exchange_1.1) | copy-start | bytes 589828
  134.7 3.0 %copy-start.6 = (bf16[8,96,768]{2,1,0:T(8,128)(2,1)S(1)}, bf16[8,96,768]{2,1,0:T(8,128)(2,1)}, u32[]{:S(2)}) copy-start(bf16[8,96,768]{2,1,0:T(8,128)(2,1)} %get-tuple-element.32) | copy-start | bytes 3538948
  136.1 1.5 copy-start.4
  158.0 2.0 copy-start.21
  158.0 2.0 copy-start.23
  160.0 0.9 copy-start.19
  160.9 0.8 copy-start.33
  161.3 0.9 copy-start.9
  161.9 1.1 copy-start.34
  162.2 0.7 copy-start.35
  162.2 1.2 copy-start.8
  162.2 1.5 copy-start.17
  162.2 1.5 copy-start.39
  162.3 1.5 copy-start.41
  168.0 1.4 copy-start.15
  168.0 1.4 copy-start.27
  227.0 1.6 copy-start.29
  228.7 1.5 copy-start.31
  230.2 1.5 copy-start.3
  230.2 1.9 copy-start.13
  230.2 2.1 copy-start.5
  230.6 2.5 %copy-start.28 = (bf16[4,96,768]{2,1,0:T(8,128)(2,1)S(1)}, bf16[4,96,768]{2,1,0:T(8,128)(2,1)}, u32[]{:S(2)}) copy-start(bf16[4,96,768]{2,1,0:T(8,128)(2,1)} %get-tuple-element.44) | copy-start | bytes 1769476
  231.7 2.3 copy-start.2
  231.7 2.3 copy-start.30
  232.3 2.4 %copy-start.37 = (f32[4,2,96]{2,1,0:T(2,128)S(1)}, f32[4,2,96]{2,1,0:T(2,128)}, u32[]{:S(2)}) copy-start(f32[4,2,96]{2,1,0:T(2,128)} %get-tuple-element.47) | copy-start | bytes 9220
